TPU v7x, 32 devices: a whole 2x2x4 slice. The times are simulated.
32 devices in a mesh: fsdp: 32 (over z, y, x, core).
Axes of the slice: x: 2, y: 2, z: 4, core: 2. Of those that a mesh axis runs over, the one named last changes fastest.
Arguments:
- images: float32 [32, 196, 512], P('fsdp'), may hold values from -40 to 40
- counts: int32 [32], P('fsdp'), may hold values from 0 to 1, as said below
- cotangent: float32 [32, 196, 512], P('fsdp'), may hold values from -40 to 40
- params: float32 [2, 3158016], P(None, 'fsdp'), may hold values from -10 to 240
- first_moment: float32 [2, 3158016], P(None, 'fsdp'), may hold values from -12 to 12
- second_moment: float32 [2, 3158016], P(None, 'fsdp'), may hold values from 1 to 100
Outputs:
- block_out: float32 [32, 196, 512], P('fsdp')
- input_grad: float32 [32, 196, 512], P('fsdp')
- param_grads: float32 [2, 3158016], P(None, 'fsdp')
- new_params: float32 [2, 3158016], P(None, 'fsdp')
- new_first: float32 [2, 3158016], P(None, 'fsdp')
- new_second: float32 [2, 3158016], P(None, 'fsdp')
Inputs may be any that keep to these rules, and one draw needn't show every extreme that they name: Each device holds counts images in its first slots; every device holds 1 or 0 images, some device holds 1 and some holds 0.
All inputs are finite; a program needn't handle non-finite values.
Results may differ from a plain program's by a relative error of at most 0.017.
Values may be sent and summed in bfloat16 or wider, within the bound.
No kernel may reach another device: no remote copies, remote signals or barrier semaphores. Data moves between devices by JAX's collectives and lax.ppermute only.
A program may use at most 192 MiB of HBM per device.

v0:
```python
import math

import jax
import jax.numpy as jnp
import numpy as np
from jax import lax
from jax.sharding import PartitionSpec as P

C = 512
HEADS = 16
FF = 2048
HEAD_DIM = 32
WIN = 7
SIDE = 14
SHIFT = 3
STEP = 3
TABLE = 169
WTOK = 49
IMG_TOK = 196


EPS_NORM = 1e-05
LEARN_RATE = 0.02
WEIGHT_DECAY = 0.1
BETA_FIRST = 0.9
BETA_SECOND = 0.95
EPS_ADAM = 1e-08
MASKED = -1e30


def entry_list():
    return (
        ("w_qkv", (C, 3 * C)),
        ("w_out", (C, C)),
        ("w_fc1", (C, FF)),
        ("w_fc2", (FF, C)),
        ("table", (TABLE, HEADS)),
        ("vectors", (8, C)),
        ("b_fc1", (FF,)),
    )


def unpack(flat_values):
    pieces = {}
    position = 0
    for entry_name, entry_shape in entry_list():
        length = math.prod(entry_shape)
        pieces[entry_name] = flat_values[position : position + length].reshape(entry_shape)
        position += length
    return pieces


def pack(pieces, total_length):
    parts_all = [pieces[entry_name].reshape(-1) for entry_name, entry_shape in entry_list()]
    used_length = sum((part.shape[0] for part in parts_all))
    parts_all.append(jnp.zeros((total_length - used_length,), jnp.float32))
    return jnp.concatenate(parts_all)


def offset_onehot():
    row_pos = np.arange(WTOK) // WIN
    col_pos = np.arange(WTOK) % WIN
    span_count = 2 * WIN - 1
    rel_index = (row_pos[:, None] - row_pos[None, :] + WIN - 1) * span_count + (
        col_pos[:, None] - col_pos[None, :] + WIN - 1
    )
    table_ids = np.arange(TABLE)
    return jnp.asarray(rel_index.reshape(-1)[:, None] == table_ids[None, :]).astype(jnp.float32)


def region_mask():
    coords = np.arange(SIDE)
    labels = (coords >= SIDE - WIN).astype(np.int64) + (coords >= SIDE - SHIFT).astype(np.int64)
    region = labels[:, None] * 3 + labels[None, :]
    grid_count = SIDE // WIN
    region = (
        region.reshape(grid_count, WIN, grid_count, WIN)
        .transpose(0, 2, 1, 3)
        .reshape(grid_count * grid_count, WTOK)
    )
    return jnp.asarray(region[:, :, None] == region[:, None, :])


def to_windows(tokens, shifted):
    count_img = tokens.shape[0]
    feature = tokens.shape[-1]
    grid_count = SIDE // WIN
    spatial = tokens.reshape(count_img, SIDE, SIDE, feature)
    if shifted:
        spatial = jnp.roll(spatial, (-SHIFT, -SHIFT), (1, 2))
    blocks = spatial.reshape(count_img, grid_count, WIN, grid_count, WIN, feature).transpose(
        0, 1, 3, 2, 4, 5
    )
    return blocks.reshape(count_img * grid_count * grid_count, WTOK, feature)


def from_windows(windows, shifted):
    grid_count = SIDE // WIN
    feature = windows.shape[-1]
    count_img = windows.shape[0] // (grid_count * grid_count)
    spatial = windows.reshape(count_img, grid_count, grid_count, WIN, WIN, feature).transpose(
        0, 1, 3, 2, 4, 5
    )
    spatial = spatial.reshape(count_img, SIDE, SIDE, feature)
    if shifted:
        spatial = jnp.roll(spatial, (SHIFT, SHIFT), (1, 2))
    return spatial.reshape(count_img, IMG_TOK, feature)


def norm_forward(stream, gain_row, shift_row):
    mean_row = jnp.mean(stream, axis=-1, keepdims=True)
    centered = stream - mean_row
    inv_std = lax.rsqrt(jnp.mean(centered * centered, axis=-1, keepdims=True) + EPS_NORM)
    normed = centered * inv_std
    return (normed, inv_std, (normed * gain_row + shift_row).astype(jnp.bfloat16))


def norm_backward(grad_hidden, normed, inv_std, gain_row):
    d_normed = grad_hidden * gain_row
    grad_in = inv_std * (
        d_normed
        - jnp.mean(d_normed, axis=-1, keepdims=True)
        - normed * jnp.mean(d_normed * normed, axis=-1, keepdims=True)
    )
    return (grad_in, jnp.sum(grad_hidden * normed, axis=0), jnp.sum(grad_hidden, axis=0))


def gelu_parts(pre_act):
    cdf_part = 0.5 * (1.0 + lax.erf(pre_act * 0.7071067811865476))
    slope_part = cdf_part + pre_act * jnp.exp(-0.5 * pre_act * pre_act) * 0.3989422804014327
    return (pre_act * cdf_part, slope_part)


def relative_bias(table_b):
    looked = jnp.dot(offset_onehot(), table_b.astype(jnp.float32), precision=lax.Precision.HIGHEST)
    return looked.reshape(WTOK, WTOK, HEADS).transpose(2, 0, 1)


def window_scores(query_b, key_b, bias_full, shifted):
    scores = (
        jnp.einsum("nqhd,nkhd->nhqk", query_b, key_b, preferred_element_type=jnp.float32)
        + bias_full[None]
    )
    if shifted:
        count_win = query_b.shape[0]
        region = jnp.tile(region_mask(), (count_win // region_mask().shape[0], 1, 1))[:, None]
        scores = jnp.where(region, scores, MASKED)
    return scores


def layer_forward(stream, weights, shifted):
    count_img = stream.shape[0]
    rows_all = count_img * IMG_TOK
    score_scale = HEAD_DIM ** (-0.5)
    vectors = weights["vectors"].astype(jnp.float32)
    stream_rows = stream.reshape(rows_all, C)
    normed_one, inv_one, hidden_one = norm_forward(stream_rows, vectors[0], vectors[1])
    windows_in = to_windows(hidden_one.reshape(count_img, IMG_TOK, C), shifted).reshape(rows_all, C)
    qkv_all = jnp.dot(windows_in, weights["w_qkv"], preferred_element_type=jnp.float32)
    head_shape = (-1, WTOK, HEADS, HEAD_DIM)
    query_b = ((qkv_all[:, :C] + vectors[2]) * score_scale).astype(jnp.bfloat16).reshape(head_shape)
    key_b = qkv_all[:, C : 2 * C].astype(jnp.bfloat16).reshape(head_shape)
    value_b = (qkv_all[:, 2 * C :] + vectors[3]).astype(jnp.bfloat16).reshape(head_shape)
    bias_full = relative_bias(weights["table"])
    scores = window_scores(query_b, key_b, bias_full, shifted)
    row_max = jnp.max(scores, axis=-1, keepdims=True)
    log_total = row_max + jnp.log(jnp.sum(jnp.exp(scores - row_max), axis=-1, keepdims=True))
    probs_b = jnp.exp(scores - log_total).astype(jnp.bfloat16)
    attended = jnp.einsum("nhqk,nkhd->nqhd", probs_b, value_b, preferred_element_type=jnp.float32)
    attended = attended.astype(jnp.bfloat16).reshape(-1, WTOK, C)
    attended_tok = from_windows(attended, shifted).reshape(rows_all, C)
    projected = (
        jnp.dot(attended_tok, weights["w_out"], preferred_element_type=jnp.float32) + vectors[4]
    )
    mid_stream = stream_rows + projected
    normed_two, inv_two, hidden_two = norm_forward(mid_stream, vectors[5], vectors[6])
    pre_act = jnp.dot(hidden_two, weights["w_fc1"], preferred_element_type=jnp.float32) + weights[
        "b_fc1"
    ].astype(jnp.float32)
    act_f, gelu_slope = gelu_parts(pre_act)
    act_b = act_f.astype(jnp.bfloat16)
    result = (
        mid_stream
        + jnp.dot(act_b, weights["w_fc2"], preferred_element_type=jnp.float32)
        + vectors[7]
    )
    kept_values = (
        normed_one,
        inv_one,
        windows_in,
        query_b,
        key_b,
        value_b,
        bias_full,
        log_total,
        attended_tok,
        normed_two,
        inv_two,
        hidden_two,
        gelu_slope,
        act_b,
    )
    return (result.reshape(count_img, IMG_TOK, C), kept_values)


def layer_backward(grad_out, kept_values, weights, shifted):
    (
        normed_one,
        inv_one,
        windows_in,
        query_b,
        key_b,
        value_b,
        bias_full,
        log_total,
        attended_tok,
        normed_two,
        inv_two,
        hidden_two,
        gelu_slope,
        act_b,
    ) = kept_values
    count_img = grad_out.shape[0]
    rows_all = count_img * IMG_TOK
    score_scale = HEAD_DIM ** (-0.5)
    vectors = weights["vectors"].astype(jnp.float32)
    grad_rows = grad_out.reshape(rows_all, C)
    grad_rows_b = grad_rows.astype(jnp.bfloat16)
    g_fc2 = jnp.dot(act_b.T, grad_rows_b, preferred_element_type=jnp.float32)
    d_pre = (
        jnp.dot(grad_rows_b, weights["w_fc2"].T, preferred_element_type=jnp.float32) * gelu_slope
    )
    d_pre_b = d_pre.astype(jnp.bfloat16)
    g_fc1 = jnp.dot(hidden_two.T, d_pre_b, preferred_element_type=jnp.float32)
    d_hidden_two = jnp.dot(d_pre_b, weights["w_fc1"].T, preferred_element_type=jnp.float32)
    d_norm_two, g_gain_two, g_shift_two = norm_backward(
        d_hidden_two, normed_two, inv_two, vectors[5]
    )
    d_mid = grad_rows + d_norm_two
    d_mid_b = d_mid.astype(jnp.bfloat16)
    g_out = jnp.dot(attended_tok.T, d_mid_b, preferred_element_type=jnp.float32)
    d_att = jnp.dot(d_mid_b, weights["w_out"].T, preferred_element_type=jnp.float32).astype(
        jnp.bfloat16
    )
    d_att_win = to_windows(d_att.reshape(count_img, IMG_TOK, C), shifted).reshape(
        -1, WTOK, HEADS, HEAD_DIM
    )
    scores = window_scores(query_b, key_b, bias_full, shifted)
    attn_probs = jnp.exp(scores - log_total)
    probs_b = attn_probs.astype(jnp.bfloat16)
    d_probs = jnp.einsum("nqhd,nkhd->nhqk", d_att_win, value_b, preferred_element_type=jnp.float32)
    d_value = jnp.einsum("nhqk,nqhd->nkhd", probs_b, d_att_win, preferred_element_type=jnp.float32)
    d_scores = attn_probs * (d_probs - jnp.sum(d_probs * attn_probs, axis=-1, keepdims=True))
    d_scores_b = d_scores.astype(jnp.bfloat16)
    d_query = (
        jnp.einsum("nhqk,nkhd->nqhd", d_scores_b, key_b, preferred_element_type=jnp.float32)
        * score_scale
    )
    d_key = jnp.einsum("nhqk,nqhd->nkhd", d_scores_b, query_b, preferred_element_type=jnp.float32)
    d_bias = jnp.sum(d_scores, axis=0).transpose(1, 2, 0).reshape(WTOK * WTOK, HEADS)
    g_table = jnp.dot(offset_onehot().T, d_bias, precision=lax.Precision.HIGHEST)
    d_query_rows = d_query.reshape(rows_all, C)
    d_value_rows = d_value.reshape(rows_all, C)
    d_qkv_b = jnp.concatenate(
        [d_query_rows, d_key.reshape(rows_all, C), d_value_rows], axis=1
    ).astype(jnp.bfloat16)
    g_qkv = jnp.dot(windows_in.T, d_qkv_b, preferred_element_type=jnp.float32)
    d_hidden_win = jnp.dot(d_qkv_b, weights["w_qkv"].T, preferred_element_type=jnp.float32)
    d_hidden_one = from_windows(d_hidden_win.reshape(-1, WTOK, C), shifted).reshape(rows_all, C)
    d_norm_one, g_gain_one, g_shift_one = norm_backward(
        d_hidden_one, normed_one, inv_one, vectors[0]
    )
    grad_in = d_mid + d_norm_one
    g_vectors = jnp.stack(
        [
            g_gain_one,
            g_shift_one,
            jnp.sum(d_query_rows, axis=0),
            jnp.sum(d_value_rows, axis=0),
            jnp.sum(d_mid, axis=0),
            g_gain_two,
            g_shift_two,
            jnp.sum(grad_rows, axis=0),
        ]
    )
    grad_terms = {
        "w_qkv": g_qkv,
        "w_out": g_out,
        "w_fc1": g_fc1,
        "w_fc2": g_fc2,
        "table": g_table,
        "vectors": g_vectors,
        "b_fc1": jnp.sum(d_pre, axis=0),
    }
    return (grad_in.reshape(count_img, IMG_TOK, C), grad_terms)


def adam_update(weights_now, grads_now, moment_one, moment_two):
    new_one = BETA_FIRST * moment_one + (1.0 - BETA_FIRST) * grads_now
    new_two = BETA_SECOND * moment_two + (1.0 - BETA_SECOND) * grads_now * grads_now
    corr_one = 1.0 - BETA_FIRST**STEP
    corr_two = 1.0 - BETA_SECOND**STEP
    update = new_one / corr_one / (jnp.sqrt(new_two / corr_two) + EPS_ADAM)
    return (weights_now - LEARN_RATE * (update + WEIGHT_DECAY * weights_now), new_one, new_two)


def fetch_weights(shard_row):
    return lax.all_gather(shard_row.astype(jnp.bfloat16), "fsdp", axis=0, tiled=True)


def reduce_both(terms_first, terms_second, shard_len):
    device_count = lax.axis_size("fsdp")
    joined = jnp.stack([terms_first, terms_second]).reshape(2, device_count, shard_len)
    joined = joined.transpose(1, 0, 2).reshape(-1)
    summed = lax.psum_scatter(joined, "fsdp", scatter_dimension=0, tiled=True)
    return summed.reshape(2, shard_len)


def local(images, counts, cotangent, params, first_moment, second_moment):
    shard_len = params.shape[1]
    flat_len = shard_len * lax.axis_size("fsdp")
    slot_valid = (jnp.arange(images.shape[0]) < counts[0]).astype(jnp.float32)[:, None, None]
    weights_one = unpack(fetch_weights(params[0]))
    weights_two = unpack(fetch_weights(params[1]))
    stream_one, kept_one = layer_forward(images, weights_one, False)
    result, kept_two = layer_forward(stream_one, weights_two, True)
    grad_mid, terms_two = layer_backward(cotangent * slot_valid, kept_two, weights_two, True)
    grad_first, terms_one = layer_backward(grad_mid, kept_one, weights_one, False)
    param_grads = reduce_both(pack(terms_one, flat_len), pack(terms_two, flat_len), shard_len)
    new_params, new_first, new_second = adam_update(
        params, param_grads, first_moment, second_moment
    )
    return (
        result * slot_valid,
        grad_first * slot_valid,
        param_grads,
        new_params,
        new_first,
        new_second,
    )


def solution(mesh):
    return jax.shard_map(
        local,
        mesh=mesh,
        in_specs=(
            P("fsdp", None, None),
            P("fsdp"),
            P("fsdp", None, None),
            P(None, "fsdp"),
            P(None, "fsdp"),
            P(None, "fsdp"),
        ),
        out_specs=(
            P("fsdp", None, None),
            P("fsdp", None, None),
            P(None, "fsdp"),
            P(None, "fsdp"),
            P(None, "fsdp"),
            P(None, "fsdp"),
        ),
        check_vma=False,
    )
```

profile of v0, /device:TPU:0, one launch (start us, length us, event | category | flops | bytes accessed | tf_op | source)
XLA Modules:
  0.0 1215.1 jit_solution(3821629834817109)
XLA Ops:
  14.0 95.5 %all-gather.5.cloned.1.call-done = bf16[1,3158016]{1,0:T(2,128)(2,1)} async-done(((bf16[1,98688]{1,0:T(2,128)(2,1)}), bf16[1,3158016]{1,0:T(2,128)(2,1)}) %all-gather.5.cloned.1.call-update) | async-done | bytes 6316048 | tf_op jit(solution)/shard_map/all_gather | solution.py:308
  110.7 27.3 %slice_reduce_fusion.5 = bf16[786432]{0:T(1024)(128)(2,1)S(1)} fusion(bf16[1,3158016]{1,0:T(2,128)(2,1)} %all-gather.5.cloned.1.call-done), kind=kLoop, calls=%fused_computation.6 | loop fusion | bytes 3145728 | tf_op jit(solution)/shard_map/slice | solution.py:48
  138.0 3.2 slice.303
  141.2 1.9 fusion.116
  151.1 1.9 add_reduce_fusion
  155.3 3.3 copy.204
  160.5 10.7 slice_reduce_fusion.7
  171.3 2.2 slice.312
  173.4 47.5 %slice_reduce_fusion.2 = (bf16[1048576]{0:T(1024)(128)(2,1)}, bf16[1048576]{0:T(1024)(128)(2,1)}) fusion(bf16[1,3158016]{1,0:T(2,128)(2,1)} %all-gather.5.cloned.1.call-done), kind=kLoop, calls=%fused_computation.3 | loop fusion | bytes 8388608 | tf_op jit(solution)/shard_map/slice | solution.py:48
  220.9 4.2 slice.317
  225.1 4.6 slice.320
  233.6 3.7 multiply_convert_fusion.1
  242.9 28.4 %slice_reduce_fusion.4 = bf16[786432]{0:T(1024)(128)(2,1)} fusion(bf16[1,3158016]{1,0:T(2,128)(2,1)} %all-gather.7.cloned.1.call-done), kind=kLoop, calls=%fused_computation.5 | loop fusion | bytes 3145728 | tf_op jit(solution)/shard_map/slice | solution.py:48
  271.3 4.6 slice.331
  275.9 1.9 fusion.117
  280.0 2.6 copy.214
  283.5 2.6 convolution_bitcast_fusion.8
  286.1 2.1 copy.213
  289.6 2.6 copy.210
  293.6 2.6 copy.211
  296.2 2.0 fusion.112
  301.3 3.3 copy.216
  308.8 4.3 reshape.678
  314.7 10.7 slice_reduce_fusion.6
  325.5 2.1 slice.344
  327.6 47.4 %slice_reduce_fusion = (bf16[1048576]{0:T(1024)(128)(2,1)}, bf16[1048576]{0:T(1024)(128)(2,1)}) fusion(bf16[1,3158016]{1,0:T(2,128)(2,1)} %all-gather.7.cloned.1.call-done), kind=kLoop, calls=%fused_computation.1 | loop fusion | bytes 8388608 | tf_op jit(solution)/shard_map/slice | solution.py:48
  375.0 4.2 slice.349
  381.0 4.7 slice.352
  386.5 3.5 multiply_convert_fusion
  403.4 2.4 reshape_reshape.39
  405.8 2.8 copy.220
  408.6 3.8 fusion.105
  417.8 2.6 copy.283
  420.4 2.5 reshape.682
  422.9 2.6 copy.282
  425.5 2.5 reshape.681
  428.0 2.6 copy.281
  430.6 2.5 reshape.680
  433.1 2.7 fusion.23
  439.5 4.3 reshape.679
  443.8 3.5 multiply_reduce_fusion.15
  451.6 1.9 fusion.96
  453.6 3.9 fusion.115
  464.3 2.4 reshape_reshape.41
  466.7 2.8 copy.236
  469.5 3.1 fusion.103
  482.0 2.8 convolution_bitcast_fusion.1
  495.1 2.8 convolution_bitcast_fusion.3
  497.9 2.7 convolution_bitcast_fusion.2
  509.8 1.9 reshape.620
  511.7 2.5 copy.311
  514.2 5.1 copy.312
  520.2 3.0 copy.313
  529.8 1.8 fusion.34
  533.5 2.5 copy.307
  536.0 5.2 copy.308
  541.2 3.0 copy.309
  546.7 4.2 multiply_reduce_fusion.2
  558.5 94.5 %concatenate.96 = f32[3158016]{0:T(1024)} concatenate(f32[786432]{0:T(1024)S(1)} %copy-done.4, f32[262144]{0:T(1024)} %bitcast.235, f32[1048576]{0:T(1024)} %bitcast.229, f32[1048576]{0:T(1024)} %bitcast.230, f32[2704]{0:T(1024)} %reshape.625, f32[4096]{0:T(1024)} %bitcast.261, f32[2048]{0:T(1024)} %get-tuple-element.121, f32[3440]{0:T(1024)} %broadcast.284), dimensions={0} | concatenate | bytes 25264128 | tf_op jit(solution)/shard_map/concatenate | solution.py:57
  653.0 103.2 %concatenate.94 = f32[3158016]{0:T(1024)} concatenate(f32[786432]{0:T(1024)} %reshape.610, f32[262144]{0:T(1024)} %bitcast.236, f32[1048576]{0:T(1024)} %bitcast.231, f32[1048576]{0:T(1024)} %bitcast.232, f32[2704]{0:T(1024)} %reshape.615, f32[4096]{0:T(1024)} %bitcast.262, f32[2048]{0:T(1024)} %get-tuple-element.123, f32[3440]{0:T(1024)} %broadcast.284), dimensions={0} | concatenate | bytes 25264128 | tf_op jit(solution)/shard_map/concatenate | solution.py:57
  756.3 25.7 %maximum_bitcast_fusion = f32[32,2,98688]{2,1,0:T(2,128)} fusion(f32[1,32,98688]{2,0,1:T(1,128)} %bitcast.227, f32[1,32,98688]{2,0,1:T(1,128)} %bitcast.228), kind=kLoop, calls=%fused_computation | loop fusion | flops 6316032 | bytes 50528256 | tf_op jit(solution)/shard_map/transpose | solution.py:314
  782.0 25.8 %reshape.627 = f32[6316032]{0:T(1024)} reshape(f32[32,2,98688]{2,1,0:T(2,128)} %maximum_bitcast_fusion) | data formatting | bytes 50528256 | tf_op jit(solution)/shard_map/reshape | solution.py:314
  813.4 388.1 %all-reduce.3.cloned.1.call-done = f32[6316032]{0:T(1024)} async-done(((f32[6316032]{0:T(1024)}), f32[6316032]{0:T(1024)}) %all-reduce.3.cloned.1.call-update) | async-done | bytes 25264144
  1203.5 4.9 multiply_subtract_fusion
  (415 shorter events, 134.5 us)
Async XLA Ops:
  7.2 3.8 copy-start.5
  7.2 102.4 %all-gather.5.cloned.1.call-start = ((), (), s32[]{:S(2)}) async-start(), calls=%async_computation | async-start | bytes 13026816 | tf_op jit(solution)/shard_map/all_gather | solution.py:308
  8.7 4.7 copy-start.35
  10.1 221.2 %all-gather.7.cloned.1.call-start = ((), (), s32[]{:S(2)}) async-start(), calls=%async_computation.1 | async-start | bytes 13026816 | tf_op jit(solution)/shard_map/all_gather | solution.py:308
  10.9 1190.6 %all-reduce.3.cloned.1.call-start = ((), (), s32[]{:S(2)}) async-start(), calls=%async_computation.2 | async-start | bytes 50528256
  12.5 98.0 %copy-start.106 = (f32[196]{0:T(256)}, f32[196]{0:T(256)S(1)}, u32[]{:S(2)}) copy-start(f32[196]{0:T(256)S(1)} %add_rsqrt_fusion.3) | copy-start | bytes 2356
  12.7 125.3 %copy-start.79 = (f32[2,7,2,7]{3,1,2,0:T(8,128)}, f32[2,7,2,7]{3,1,2,0:T(8,128)S(1)}, u32[]{:S(2)}) copy-start(f32[2,7,2,7]{3,1,2,0:T(8,128)S(1)} %copy.194) | copy-start | bytes 2356
  12.7 125.3 %copy-start.80 = (f32[2,7,2,7]{3,1,2,0:T(8,128)}, f32[2,7,2,7]{3,1,2,0:T(8,128)S(1)}, u32[]{:S(2)}) copy-start(f32[2,7,2,7]{3,1,2,0:T(8,128)S(1)} %copy.192) | copy-start | bytes 2356
  110.4 27.6 %copy-start.98 = (f32[1,512]{1,0:T(1,128)}, f32[1,512]{1,0:T(1,128)S(1)}, u32[]{:S(2)}) copy-start(f32[1,512]{1,0:T(1,128)S(1)} %get-tuple-element.95) | copy-start | bytes 6148
  110.4 123.2 %copy-start.70 = (f32[1,512]{1,0:T(1,128)}, f32[1,512]{1,0:T(1,128)S(1)}, u32[]{:S(2)}) copy-start(f32[1,512]{1,0:T(1,128)S(1)} %get-tuple-element.90) | copy-start | bytes 6148
  110.4 123.2 %copy-start.75 = (f32[1,512]{1,0:T(1,128)}, f32[1,512]{1,0:T(1,128)S(1)}, u32[]{:S(2)}) copy-start(f32[1,512]{1,0:T(1,128)S(1)} %get-tuple-element.89) | copy-start | bytes 6148
  110.7 30.5 %copy-start.55 = (bf16[196,512]{1,0:T(8,128)(2,1)}, bf16[196,512]{1,0:T(8,128)(2,1)S(1)}, u32[]{:S(2)}) copy-start(bf16[196,512]{1,0:T(8,128)(2,1)S(1)} %reshape_reshape.32) | copy-start | bytes 602116
  138.0 5.1 copy-start.3
  154.0 4.6 copy-start.60
  160.5 69.2 %copy-start.52 = (bf16[196,512]{1,0:T(8,128)(2,1)}, bf16[196,512]{1,0:T(8,128)(2,1)S(1)}, u32[]{:S(2)}) copy-start(bf16[196,512]{1,0:T(8,128)(2,1)S(1)} %reshape_reshape_reshape.10) | copy-start | bytes 602116
  231.1 6.3 copy-start.83
  231.3 6.0 copy-start.93
  232.8 5.7 copy-start.81
  233.6 3.8 copy-start.45
  242.8 33.1 %copy-start.56 = (bf16[196,512]{1,0:T(8,128)(2,1)}, bf16[196,512]{1,0:T(8,128)(2,1)S(1)}, u32[]{:S(2)}) copy-start(bf16[196,512]{1,0:T(8,128)(2,1)S(1)} %reshape_reshape.35) | copy-start | bytes 602116
  286.1 6.1 copy-start.68
  289.6 6.6 copy-start.90
  375.0 4.2 copy-start.113
  380.7 12.4 %copy-start.86 = (f32[196]{0:T(256)}, f32[196]{0:T(256)S(1)}, u32[]{:S(2)}) copy-start(f32[196]{0:T(256)S(1)} %broadcast_multiply_fusion.8) | copy-start | bytes 2356
  380.9 12.2 %copy-start.96 = (f32[196]{0:T(256)}, f32[196]{0:T(256)S(1)}, u32[]{:S(2)}) copy-start(f32[196]{0:T(256)S(1)} %add_rsqrt_fusion) | copy-start | bytes 2356
  380.9 5.5 copy-start.73
  380.9 5.5 copy-start.77
  399.2 9.4 copy-start.63
  408.6 3.8 copy-start.1
  408.6 3.8 copy-start.26
  408.6 3.8 copy-start.27
  438.2 5.6 copy-start.82
  439.5 9.6 copy-start.92
  439.5 9.6 copy-start.101
  453.6 5.4 copy-start.33
  453.6 3.9 copy-start.7
  453.6 3.9 copy-start.71
  453.6 3.9 copy-start.84
  453.6 3.9 copy-start.94
  459.8 33.8 %copy-start.13 = (f32[196,512]{1,0:T(8,128)}, f32[196,512]{1,0:T(8,128)S(1)}, u32[]{:S(2)}) copy-start(f32[196,512]{1,0:T(8,128)S(1)} %get-tuple-element.55) | copy-start | bytes 1204228
  460.8 8.7 copy-start.61
  478.2 3.8 copy-start.65
  478.2 3.8 copy-start.74
  478.2 3.8 copy-start.78
  478.2 3.8 copy-start.87
  478.2 3.8 copy-start.97
  489.6 4.1 copy-start.53
  490.8 4.2 copy-start.67
  490.8 4.2 copy-start.72
  490.8 4.2 copy-start.76
  490.8 4.2 copy-start.85
  490.8 4.2 copy-start.95
  497.9 4.2 copy-start.39
  500.6 4.3 copy-start.49
  502.1 3.9 copy-start.50
  514.2 5.2 copy-start.9
  514.2 5.2 copy-start.37
  523.6 4.2 copy-start.47
  523.8 5.0 copy-start.48
  536.0 5.3 copy-start.2
  546.7 11.9 copy-start.4
  812.2 391.2 %copy-start.41 = (f32[2,98688]{1,0:T(2,128)S(1)}, f32[2,98688]{1,0:T(2,128)}, u32[]{:S(2)}) copy-start(f32[2,98688]{1,0:T(2,128)} %param.15) | copy-start | bytes 2368516
  812.2 391.2 %copy-start.69 = (f32[2,98688]{1,0:T(2,128)S(1)}, f32[2,98688]{1,0:T(2,128)}, u32[]{:S(2)}) copy-start(f32[2,98688]{1,0:T(2,128)} %param.16) | copy-start | bytes 2368516
  1203.5 4.9 copy-start.42
  (59 other events, 132.0 us)
Sparse Core Ops, SparseCore 0:
  11.4 98.1 all-gather.4
  112.9 93.9 all-gather.6
  808.0 393.4 all-reduce.2
where the time goes:
time: 1240 us; the launch traced here: 1220 us
  local copies, waits for them, and re-layouts  582 us (47%)
  waiting for transfers between devices  484 us (39%)
  matrix products  74 us (6%)
  other arithmetic  58.9 us (5%)
  between operations  16 us (1%)
    unnamed x4, waiting for transfers between devices  389 us
    slice x20, local copies, waits for them, and re-layouts, unpack(): flat_values[position:position + length].reshape(entry_shape)  212 us
    concatenate x2, local copies, waits for them, and re-layouts, pack(): return jnp.concatenate(parts_all)  198 us
    all_gather x2, waiting for transfers between devices, fetch_weights(): lax.all_gather(shard_row.astype(jnp.bfloat16), 'fsdp', axis=0, tiled=True)  95.5 us
    unnamed x251, local copies, waits for them, and re-layouts  33.5 us
    reshape x1, local copies, waits for them, and re-layouts, reduce_both(): joined = joined.transpose(1, 0, 2).reshape(-1)  25.8 us
    transpose x1, other arithmetic, reduce_both(): joined = joined.transpose(1, 0, 2).reshape(-1)  25.7 us
  transfers between devices with their start and end apart: 3, of which 2 were waited for; matrix products, arithmetic and copies ran while one was open for 10% of the time, Pallas kernels for 0%

commit v1 on v0

v1 whole, which is shorter than its diff:
```python
import functools
import math

import jax
import jax.numpy as jnp
import numpy as np
from jax import lax
from jax.experimental import pallas as pl
from jax.experimental.pallas import tpu as pltpu
from jax.sharding import Mesh
from jax.sharding import PartitionSpec as P

C = 512
HEADS = 16
FF = 2048
HEAD_DIM = 32
WIN = 7
SIDE = 14
SHIFT = 3
STEP = 3
TABLE = 169
WTOK = 49
IMG_TOK = 196

EPS_NORM = 1e-05
LEARN_RATE = 0.02
WEIGHT_DECAY = 0.1
BETA_FIRST = 0.9
BETA_SECOND = 0.95
EPS_ADAM = 1e-08
MASKED = -1e30

LANES = 128
NWIN = 4
WPAD = 64
ROWS = NWIN * WPAD
TPAD = 176
TOUT = 200

BASE_QKV, PITCH_QKV = 0, 12
BASE_OUT, PITCH_OUT = 6144, 4
BASE_FC1, PITCH_FC1 = 8192, 16
BASE_FC2, PITCH_FC2 = 16384, 4
BASE_TAIL = 24576
TAIL_VEC = 21
VEC_SKIP = 16
VEC_ROWS = 48

F32 = jnp.float32
BF16 = jnp.bfloat16


def round_up(value, unit):
    return (value + unit - 1) // unit * unit


def window_index(shifted):
    index = np.full((ROWS,), -1, np.int64)
    for wi in range(2):
        for wj in range(2):
            for ra in range(WIN):
                for ca in range(WIN):
                    i, j = wi * WIN + ra, wj * WIN + ca
                    if shifted:
                        i, j = (i + SHIFT) % SIDE, (j + SHIFT) % SIDE
                    index[(wi * 2 + wj) * WPAD + ra * WIN + ca] = i * SIDE + j
    return index


def order_matrices():
    first, second = window_index(False), window_index(True)
    take_first = np.zeros((ROWS, ROWS), np.float32)
    take_second = np.zeros((ROWS, ROWS), np.float32)
    for row in range(ROWS):
        if first[row] >= 0:
            take_first[row, first[row]] = 1.0
        if second[row] >= 0:
            take_second[row, second[row]] = 1.0
    return take_first, take_second


def key_masks():
    coords = np.arange(SIDE)
    labels = (coords >= SIDE - WIN).astype(np.int64) + (coords >= SIDE - SHIFT).astype(np.int64)
    region = labels[:, None] * 3 + labels[None, :]
    region = region.reshape(2, WIN, 2, WIN).transpose(0, 2, 1, 3).reshape(NWIN, WTOK)
    masks = np.zeros((2, NWIN, WPAD, WPAD), np.float32)
    masks[:, :, :, WTOK:] = MASKED
    masks[1, :, :WTOK, :WTOK] = np.where(region[:, :, None] == region[:, None, :], 0.0, MASKED)
    return np.concatenate([masks, masks], axis=-1)


def table_constants():
    offset = np.arange(TPAD)
    rows = (offset[:, None] // 8 == np.arange(24)[None, :]).astype(np.float32)
    lane = np.arange(LANES)
    lane_mask = (offset[:, None] % 8 == lane[None, :] // 16).astype(np.float32)
    order = np.concatenate([np.arange(0, HEADS, 2), np.arange(1, HEADS, 2)])
    heads = (lane[None, :] % 16 == order[:, None]).astype(np.float32)
    return rows, lane_mask, heads


def offset_lanes():
    lane = lax.broadcasted_iota(jnp.int32, (TPAD, WTOK, LANES), 2) % WPAD
    query = lax.broadcasted_iota(jnp.int32, (TPAD, WTOK, LANES), 1)
    want = lax.broadcasted_iota(jnp.int32, (TPAD, WTOK, LANES), 0)
    span = 2 * WIN - 1
    have = (query // WIN - lane // WIN + WIN - 1) * span + (query % WIN - lane % WIN + WIN - 1)
    hit = (have == want) & (lane < WTOK)
    return hit.astype(BF16).reshape(TPAD, WTOK * LANES)


def dot(a, b):
    return lax.dot_general(a, b, (((1,), (0,)), ((), ())), preferred_element_type=F32)


def dot_nt(a, b):
    return lax.dot_general(a, b, (((1,), (1,)), ((), ())), preferred_element_type=F32)


def dot_tn(a, b):
    return lax.dot_general(a, b, (((0,), (0,)), ((), ())), preferred_element_type=F32)


def select_rows(onehot, values):
    high = values.astype(BF16)
    rest = values - high.astype(F32)
    middle = rest.astype(BF16)
    low = (rest - middle.astype(F32)).astype(BF16)
    return dot(onehot, high) + dot(onehot, middle) + dot(onehot, low)


def flat_to_staging(flat_ref, block, staging, device_count, shard_rows):
    group = 8

    @pl.loop(0, device_count // group)
    def _(step):
        view = staging.at[pl.ds(pl.multiple_of(step * group * shard_rows, 8), group * shard_rows), :]
        for i in range(group):
            view[i * shard_rows : (i + 1) * shard_rows, :] = flat_ref[
                step * group + i, block, :shard_rows, :
            ].astype(F32)


def staging_to_flat(staging, flat_ref, device_count, shard_rows, padded_rows):
    group = 8

    @pl.loop(0, device_count // group)
    def _(step):
        view = staging.at[pl.ds(pl.multiple_of(step * group * shard_rows, 8), group * shard_rows), :]
        for i in range(group):
            flat_ref[step * group + i, :shard_rows, :] = view[
                i * shard_rows : (i + 1) * shard_rows, :
            ].astype(BF16)
            if padded_rows > shard_rows:
                flat_ref[step * group + i, shard_rows:, :] = jnp.zeros(
                    (padded_rows - shard_rows, LANES), BF16
                )


def unpack_matrix(staging, target, base, pitch, chunk):
    rows = target.shape[0]

    @pl.loop(0, rows // chunk)
    def _(step):
        start = pl.multiple_of(base + step * (chunk * pitch), 8)
        view = staging.at[pl.ds(start, chunk * pitch), :]
        row = pl.multiple_of(step * chunk, chunk)
        for j in range(pitch):
            target[pl.ds(row, chunk), j * LANES : (j + 1) * LANES] = view[
                pl.ds(j, chunk, stride=pitch), :
            ].astype(BF16)


def pack_matrix(staging, values, base, pitch, first_col):
    rows, cols = values.shape
    view = staging.at[pl.ds(base, rows * pitch), :]
    for j in range(cols // LANES):
        view[pl.ds(first_col + j, rows, stride=pitch), :] = values[:, j * LANES : (j + 1) * LANES]


def lane_ids(shape):
    return lax.broadcasted_iota(jnp.int32, shape, len(shape) - 1)


def unpack_tail(staging, shift_ref, tail_rows):
    tail = staging[BASE_TAIL : BASE_TAIL + 96, :]
    shift_ref[...] = pltpu.roll(tail, LANES - VEC_SKIP, 1)
    low = shift_ref[TAIL_VEC : TAIL_VEC + VEC_ROWS, :]
    high = shift_ref[TAIL_VEC + 1 : TAIL_VEC + 1 + VEC_ROWS, :]
    joined = jnp.where(lane_ids((VEC_ROWS, LANES)) < LANES - VEC_SKIP, low, high)
    vectors = [
        jnp.concatenate([joined[4 * v + i : 4 * v + i + 1, :] for i in range(4)], axis=1)
        for v in range(8)
    ]
    b_fc1 = jnp.concatenate([joined[32 + i : 33 + i, :] for i in range(16)], axis=1)
    return vectors, b_fc1


def build_bias(staging, rows_ref, lane_mask_ref, heads_ref, offsets_ref, bias_ref):
    block = staging[BASE_TAIL : BASE_TAIL + 24, :].astype(BF16)
    spread = dot(rows_ref[...], block) * lane_mask_ref[...].astype(F32)
    table = dot_nt(heads_ref[...], spread.astype(BF16)).astype(BF16)
    bias_ref[...] = jnp.zeros_like(bias_ref)
    even = lane_ids((8, LANES)) < WPAD
    for a in range(WTOK):
        both = dot(table, offsets_ref[:, a * LANES : (a + 1) * LANES])
        bias_ref[pl.ds(a, 8, stride=WPAD), :] = jnp.where(even, both[:8], both[8:])


def norm_rows(values):
    mean = jnp.mean(values, axis=-1, keepdims=True)
    centered = values - mean
    inv_std = lax.rsqrt(jnp.mean(centered * centered, axis=-1, keepdims=True) + EPS_NORM)
    return centered * inv_std, inv_std


def norm_grad(grad_hidden, normed, inv_std, gain_row):
    d_normed = grad_hidden * gain_row
    grad_in = inv_std * (
        d_normed
        - jnp.mean(d_normed, axis=-1, keepdims=True)
        - normed * jnp.mean(d_normed * normed, axis=-1, keepdims=True)
    )
    return (
        grad_in,
        jnp.sum(grad_hidden * normed, axis=0, keepdims=True),
        jnp.sum(grad_hidden, axis=0, keepdims=True),
    )


def erf(x):
    return lax.erf(x)


def pair_masks():
    lane = lane_ids((1, 256))
    pair = [(lane // 64 == h).astype(F32).astype(BF16) for h in range(4)]
    even = (lane % 64 < 32).astype(F32).astype(BF16)
    odd = (lane % 64 >= 32).astype(F32).astype(BF16)
    pair_f = [(lane // 64 == h).astype(F32) for h in range(4)]
    return pair, even, odd, pair_f


def stack_pairs(values, pair):
    return jnp.concatenate([values * pair[h] for h in range(4)], axis=0)


def stack_halves(values, even, odd):
    return jnp.concatenate([values * even, values * odd], axis=0)


def gather_pairs(values, pair_f):
    total = values[:WPAD] * pair_f[0]
    for h in range(1, 4):
        total = total + values[h * WPAD : (h + 1) * WPAD] * pair_f[h]
    return total


def half_sum(values, even_lane):
    left = jnp.sum(jnp.where(even_lane, values, 0.0), axis=-1, keepdims=True)
    right = jnp.sum(jnp.where(even_lane, 0.0, values), axis=-1, keepdims=True)
    return left, right


def block_forward(x, w, vec, b_fc1, bias_ref, mask_ref, kept):
    normed, inv_std = norm_rows(x)
    kept["n1"][...] = normed
    kept["r1"][...] = jnp.broadcast_to(inv_std, (ROWS, LANES))
    kept["h1"][...] = (normed * vec[0] + vec[1]).astype(BF16)
    scale = HEAD_DIM ** (-0.5)
    hidden = kept["h1"][...]
    kept["q"][...] = ((dot(hidden, w["qkv"][:, :C]) + vec[2]) * scale).astype(BF16)
    kept["k"][...] = dot(hidden, w["qkv"][:, C : 2 * C]).astype(BF16)
    kept["v"][...] = (dot(hidden, w["qkv"][:, 2 * C :]) + vec[3]).astype(BF16)

    @pl.loop(0, NWIN)
    def _(win):
        pair, even, odd, pair_f = pair_masks()
        even_lane = lane_ids((1, LANES)) < WPAD
        rows = pl.ds(pl.multiple_of(win * WPAD, WPAD), WPAD)
        mask = jnp.concatenate([mask_ref[win]] * 4, axis=0)
        for g in range(2):
            cols = slice(g * 256, (g + 1) * 256)
            query = stack_pairs(kept["q"][rows, cols], pair)
            key = stack_halves(kept["k"][rows, cols], even, odd)
            value = stack_halves(kept["v"][rows, cols], even, odd)
            scores = dot_nt(query, key) + bias_ref[cols, :] + mask
            left = jnp.max(jnp.where(even_lane, scores, -3e38), axis=-1, keepdims=True)
            right = jnp.max(jnp.where(even_lane, -3e38, scores), axis=-1, keepdims=True)
            expo = jnp.exp(scores - jnp.where(even_lane, left, right))
            left, right = half_sum(expo, even_lane)
            probs = expo * jnp.where(even_lane, 1.0 / left, 1.0 / right)
            kept["p"][win * 2 + g] = probs
            mixed = dot(probs.astype(BF16), value)
            kept["att"][rows, cols] = gather_pairs(mixed, pair_f).astype(BF16)

    mid = x + dot(kept["att"][...], w["out"][...]) + vec[4]
    normed, inv_std = norm_rows(mid)
    kept["n2"][...] = normed
    kept["r2"][...] = jnp.broadcast_to(inv_std, (ROWS, LANES))
    kept["h2"][...] = (normed * vec[5] + vec[6]).astype(BF16)
    result = mid + vec[7]
    for f in range(4):
        cols = slice(f * 512, (f + 1) * 512)
        pre = dot(kept["h2"][...], w["fc1"][:, cols]) + b_fc1[:, cols]
        cdf = 0.5 * (1.0 + erf(pre * 0.7071067811865476))
        slope = cdf + pre * jnp.exp(-0.5 * pre * pre) * 0.3989422804014327
        kept["slope"][:, cols] = slope.astype(kept["slope"].dtype)
        act = (pre * cdf).astype(BF16)
        kept["act"][:, cols] = act
        result = result + dot(act, w["fc2"][cols, :])
    return result


def block_backward(dout, w, gain_one, gain_two, kept, staging, consts, scratch, device_count, shard_rows):
    rows_ref, lane_mask_ref, heads_ref, offsets_ref = consts
    datt_ref, dqkv_ref, dbias_ref, spread_hi, spread_lo, vec_rows = scratch
    grads = [None] * 8
    dout_b = dout.astype(BF16)
    grads[7] = jnp.sum(dout, axis=0, keepdims=True)
    g_b1 = []
    d_hidden = None
    for f in range(4):
        cols = slice(f * 512, (f + 1) * 512)
        pack_matrix(staging, dot_tn(kept["act"][:, cols], dout_b), BASE_FC2 + f * 512 * PITCH_FC2, PITCH_FC2, 0)
        d_pre = dot_nt(dout_b, w["fc2"][cols, :]) * kept["slope"][:, cols].astype(F32)
        g_b1.append(jnp.sum(d_pre, axis=0, keepdims=True))
        d_pre_b = d_pre.astype(BF16)
        pack_matrix(staging, dot_tn(kept["h2"][...], d_pre_b), BASE_FC1, PITCH_FC1, f * 4)
        term = dot_nt(d_pre_b, w["fc1"][:, cols])
        d_hidden = term if d_hidden is None else d_hidden + term
    d_norm, grads[5], grads[6] = norm_grad(d_hidden, kept["n2"][...], kept["r2"][:, :1], gain_two)
    d_mid = dout + d_norm
    d_mid_b = d_mid.astype(BF16)
    grads[4] = jnp.sum(d_mid, axis=0, keepdims=True)
    pack_matrix(staging, dot_tn(kept["att"][...], d_mid_b), BASE_OUT, PITCH_OUT, 0)
    datt_ref[...] = dot_nt(d_mid_b, w["out"][...]).astype(BF16)
    dbias_ref[...] = jnp.zeros_like(dbias_ref)
    vec_rows[0:16, :] = jnp.zeros((16, C), F32)
    scale = HEAD_DIM ** (-0.5)

    @pl.loop(0, NWIN)
    def _(win):
        pair, even, odd, pair_f = pair_masks()
        even_lane = lane_ids((1, LANES)) < WPAD
        even_col = lane_ids((1, 256)) % 64 < 32
        rows = pl.ds(pl.multiple_of(win * WPAD, WPAD), WPAD)
        for g in range(2):
            cols = slice(g * 256, (g + 1) * 256)
            query = stack_pairs(kept["q"][rows, cols], pair)
            key = stack_halves(kept["k"][rows, cols], even, odd)
            value = stack_halves(kept["v"][rows, cols], even, odd)
            d_att = stack_pairs(datt_ref[rows, cols], pair)
            probs = kept["p"][win * 2 + g]
            d_probs = dot_nt(d_att, value)
            left, right = half_sum(d_probs * probs, even_lane)
            d_scores = probs * (d_probs - jnp.where(even_lane, left, right))
            dbias_ref[cols, :] += d_scores
            d_scores_b = d_scores.astype(BF16)
            d_query = gather_pairs(dot(d_scores_b, key), pair_f) * scale
            d_key = dot_tn(d_scores_b, query)
            d_value = dot_tn(probs.astype(BF16), d_att)
            d_key = jnp.where(even_col, d_key[:WPAD], d_key[WPAD:])
            d_value = jnp.where(even_col, d_value[:WPAD], d_value[WPAD:])
            vec_rows[0:1, cols] += jnp.sum(d_query, axis=0, keepdims=True)
            vec_rows[8:9, cols] += jnp.sum(d_value, axis=0, keepdims=True)
            dqkv_ref[rows, cols] = d_query.astype(BF16)
            dqkv_ref[rows, C + g * 256 : C + (g + 1) * 256] = d_key.astype(BF16)
            dqkv_ref[rows, 2 * C + g * 256 : 2 * C + (g + 1) * 256] = d_value.astype(BF16)

    grads[2] = vec_rows[0:1, :]
    grads[3] = vec_rows[8:9, :]
    d_hidden = None
    for f in range(3):
        cols = slice(f * 512, (f + 1) * 512)
        pack_matrix(staging, dot_tn(kept["h1"][...], dqkv_ref[:, cols]), BASE_QKV, PITCH_QKV, f * 4)
        term = dot_nt(dqkv_ref[:, cols], w["qkv"][:, cols])
        d_hidden = term if d_hidden is None else d_hidden + term
    d_norm, grads[0], grads[1] = norm_grad(d_hidden, kept["n1"][...], kept["r1"][:, :1], gain_one)
    d_in = d_mid + d_norm

    even = lane_ids((8, LANES)) < WPAD
    for a in range(WTOK):
        part = dbias_ref[pl.ds(a, 8, stride=WPAD), :]
        part = jnp.concatenate([jnp.where(even, part, 0.0), jnp.where(even, 0.0, part)], axis=0)
        high = part.astype(BF16)
        spread_hi[:, a * LANES : (a + 1) * LANES] = high
        spread_lo[:, a * LANES : (a + 1) * LANES] = (part - high.astype(F32)).astype(BF16)
    g_table = dot_nt(offsets_ref[...], spread_hi[...]) + dot_nt(offsets_ref[...], spread_lo[...])
    g_lanes = dot(g_table.astype(BF16), heads_ref[...]) * lane_mask_ref[...].astype(F32)
    g_rows = dot_tn(rows_ref[...], g_lanes.astype(BF16))
    tail_rows = device_count * shard_rows - BASE_TAIL
    staging[BASE_TAIL : BASE_TAIL + tail_rows, :] = jnp.zeros((tail_rows, LANES), F32)
    staging[BASE_TAIL : BASE_TAIL + 24, :] = g_rows
    lines = []
    for v in range(8):
        lines += [grads[v][:, i * LANES : (i + 1) * LANES] for i in range(4)]
    for part in g_b1:
        lines += [part[:, i * LANES : (i + 1) * LANES] for i in range(4)]
    rolled = pltpu.roll(jnp.concatenate(lines, axis=0), VEC_SKIP, 1)
    first = lane_ids((VEC_ROWS, LANES)) < VEC_SKIP
    low = BASE_TAIL + TAIL_VEC
    staging[low : low + VEC_ROWS, :] += jnp.where(first, 0.0, rolled)
    staging[low + 1 : low + 1 + VEC_ROWS, :] += jnp.where(first, rolled, 0.0)
    return d_in


KEPT = {
    "n1": ((ROWS, C), F32),
    "r1": ((ROWS, LANES), F32),
    "h1": ((ROWS, C), BF16),
    "q": ((ROWS, C), BF16),
    "k": ((ROWS, C), BF16),
    "v": ((ROWS, C), BF16),
    "p": ((2 * NWIN, 256, LANES), F32),
    "att": ((ROWS, C), BF16),
    "n2": ((ROWS, C), F32),
    "r2": ((ROWS, LANES), F32),
    "h2": ((ROWS, C), BF16),
    "slope": ((ROWS, FF), F32),
    "act": ((ROWS, FF), BF16),
}
WEIGHTS = {
    "qkv": ((C, 3 * C), BF16),
    "out": ((C, C), BF16),
    "fc1": ((C, FF), BF16),
    "fc2": ((FF, C), BF16),
}
BACK_SCRATCH = [
    pltpu.VMEM((ROWS, C), BF16),
    pltpu.VMEM((ROWS, 3 * C), BF16),
    pltpu.VMEM((512, LANES), F32),
    pltpu.VMEM((16, WTOK * LANES), BF16),
    pltpu.VMEM((16, WTOK * LANES), BF16),
    pltpu.VMEM((16, C), F32),
]


def unpack_weights(flat_ref, block, staging, w, device_count, shard_rows):
    flat_to_staging(flat_ref, block, staging, device_count, shard_rows)
    unpack_matrix(staging, w["qkv"], BASE_QKV, PITCH_QKV, 128)
    unpack_matrix(staging, w["out"], BASE_OUT, PITCH_OUT, 128)
    unpack_matrix(staging, w["fc1"], BASE_FC1, PITCH_FC1, 128)
    unpack_matrix(staging, w["fc2"], BASE_FC2, PITCH_FC2, 256)


def first_kernel(sizes, *refs):
    device_count, shard_rows, padded_rows = sizes
    flat, images, order, mask, rows_c, lane_c, heads_c, offsets = refs[:8]
    names = list(KEPT) + list(WEIGHTS)
    stream, vec_out, *outs = refs[8 : 10 + len(names)]
    staging, shift, bias = refs[10 + len(names) :]
    kept = dict(zip(names, outs))
    unpack_weights(flat, 0, staging, kept, device_count, shard_rows)
    vec, b_fc1 = unpack_tail(staging, shift, None)
    vec_out[...] = jnp.concatenate(vec, axis=0)
    build_bias(staging, rows_c, lane_c, heads_c, offsets, bias)
    x = select_rows(order[...], images[...])
    stream[...] = block_forward(x, kept, vec, b_fc1, bias, mask, kept)


def second_kernel(sizes, *refs):
    device_count, shard_rows, padded_rows = sizes
    valid, flat, stream, cotangent, order, between, mask, rows_c, lane_c, heads_c, offsets = refs[:11]
    block_out, d_stream, grads = refs[11:14]
    names = list(KEPT) + list(WEIGHTS)
    kept = dict(zip(names, refs[14 : 14 + len(names)]))
    staging, shift, bias, *scratch = refs[14 + len(names) :]
    unpack_weights(flat, 0, staging, kept, device_count, shard_rows)
    vec, b_fc1 = unpack_tail(staging, shift, None)
    build_bias(staging, rows_c, lane_c, heads_c, offsets, bias)
    factor = (valid[0] > 0).astype(F32)
    x = select_rows(between[...], stream[...])
    result = block_forward(x, kept, vec, b_fc1, bias, mask, kept)
    back = order[...].T
    block_out[...] = select_rows(back, result)[:IMG_TOK] * factor
    dout = select_rows(order[...], cotangent[...]) * factor
    d_in = block_backward(
        dout, kept, vec[0], vec[5], kept, staging, (rows_c, lane_c, heads_c, offsets), scratch,
        device_count, shard_rows,
    )
    d_stream[...] = select_rows(between[...].T, d_in)
    staging_to_flat(staging, grads, device_count, shard_rows, padded_rows)


def third_kernel(sizes, *refs):
    device_count, shard_rows, padded_rows = sizes
    valid, d_stream, vec, order, rows_c, lane_c, heads_c, offsets = refs[:8]
    names = list(KEPT) + list(WEIGHTS)
    kept = dict(zip(names, refs[8 : 8 + len(names)]))
    input_grad, grads = refs[8 + len(names) : 10 + len(names)]
    staging, *scratch = refs[10 + len(names) :]
    factor = (valid[0] > 0).astype(F32)
    d_in = block_backward(
        d_stream[...], kept, vec[0:1, :], vec[5:6, :], kept, staging,
        (rows_c, lane_c, heads_c, offsets), scratch, device_count, shard_rows,
    )
    input_grad[...] = select_rows(order[...].T, d_in)[:IMG_TOK] * factor
    staging_to_flat(staging, grads, device_count, shard_rows, padded_rows)


VMEM_SPEC = pl.BlockSpec(memory_space=pltpu.VMEM)
SMEM_SPEC = pl.BlockSpec(memory_space=pltpu.SMEM)
PARAMS = pltpu.CompilerParams(vmem_limit_bytes=60 * 1024 * 1024)


def shapes_of(table):
    return [jax.ShapeDtypeStruct(shape, kind) for shape, kind in table.values()]


def scratch_of(table):
    return [pltpu.VMEM(shape, kind) for shape, kind in table.values()]


def axes_of(mesh):
    devices = list(mesh.devices.flat)
    coords = np.array([tuple(d.coords) + (d.core_on_chip,) for d in devices])
    extent = coords.max(axis=0) - coords.min(axis=0) + 1
    return int(extent[2]), int(extent[1]), int(extent[0]), int(extent[3])


def flip(values, axis):
    return lax.ppermute(values, axis, [(0, 1), (1, 0)])


def pick(values, dim, index):
    return lax.dynamic_index_in_dim(values, index, axis=dim, keepdims=False)


def reduce_rows(grads, sizes):
    names = ("z", "y", "x", "c")
    parts = [g.reshape(tuple(sizes) + g.shape[1:]) for g in grads]
    def halve(values, dim, name, size, bit):
        place = lax.axis_index(name)
        step = 1 << bit
        low = (place // step) % 2
        span = values.shape[dim]
        shaped = values.reshape(values.shape[:dim] + (span // 2, 2) + values.shape[dim + 1 :])
        sent = pick(shaped, dim + 1, 1 - low)
        pairs = [(i, i ^ step) for i in range(size)]
        return pick(shaped, dim + 1, low) + lax.ppermute(sent, name, pairs)

    def along(values, dim, name, size):
        bit = 0
        while (1 << bit) < size:
            values = halve(values, dim, name, size, bit)
            bit += 1
        return values

    z, y, x, c = sizes
    parts = [along(p, 3, "c", c) for p in parts]
    rows = parts[0].shape[4]
    cut = rows // 2 // 16 * 16
    first = [p[..., :cut, :] for p in parts]
    second = [p[..., cut:, :] for p in parts]
    first = [along(p, 2, "x", x) for p in first]
    second = [along(p, 1, "y", y) for p in second]
    first = [along(p, 1, "y", y) for p in first]
    second = [along(p, 2, "x", x) for p in second]
    parts = [jnp.concatenate([a, b], axis=4) for a, b in zip(first, second)]
    parts = [along(p, 0, "z", z) for p in parts]
    return [p.reshape(p.shape[4:]) for p in parts]


def adam_update(weights_now, grads_now, moment_one, moment_two):
    new_one = BETA_FIRST * moment_one + (1.0 - BETA_FIRST) * grads_now
    new_two = BETA_SECOND * moment_two + (1.0 - BETA_SECOND) * grads_now * grads_now
    corr_one = 1.0 - BETA_FIRST**STEP
    corr_two = 1.0 - BETA_SECOND**STEP
    update = new_one / corr_one / (jnp.sqrt(new_two / corr_two) + EPS_ADAM)
    return (weights_now - LEARN_RATE * (update + WEIGHT_DECAY * weights_now), new_one, new_two)


def local(sizes, images, counts, cotangent, params, first_moment, second_moment):
    device_count = math.prod(sizes)
    shard_len = params.shape[1]
    shard_rows = shard_len // LANES
    padded_rows = round_up(shard_rows, 16)
    dims = (device_count, shard_rows, padded_rows)
    flat_rows = device_count * shard_rows

    take_first, take_second = order_matrices()
    order_first = jnp.asarray(take_first[:, :], BF16)
    order_second = jnp.asarray(take_second, BF16)
    between = jnp.asarray(take_second @ take_first.T, BF16)
    masks = key_masks()
    mask_first, mask_second = jnp.asarray(masks[0]), jnp.asarray(masks[1])
    consts = [jnp.asarray(a, BF16) for a in table_constants()] + [offset_lanes()]

    shard = params.astype(BF16).reshape(2, shard_rows, LANES)
    shard = jnp.pad(shard, ((0, 0), (0, padded_rows - shard_rows), (0, 0)))
    axes = ("z", "y", "x", "c")
    flat_one = lax.all_gather(shard[0:1], axes, axis=0, tiled=False)
    flat_two = lax.all_gather(shard[1:2], axes, axis=0, tiled=False)

    pad_tokens = ((0, ROWS - IMG_TOK), (0, 0))
    image_rows = jnp.pad(images.reshape(IMG_TOK, C), pad_tokens)
    cot_rows = jnp.pad(cotangent.reshape(IMG_TOK, C), pad_tokens)

    grad_shape = jax.ShapeDtypeStruct((device_count, padded_rows, LANES), BF16)
    names = len(KEPT) + len(WEIGHTS)
    staging = pltpu.VMEM((flat_rows, LANES), F32)
    common = [staging, pltpu.VMEM((96, LANES), F32), pltpu.VMEM((512, LANES), F32)]
    stream, vec, *kept = pl.pallas_call(
        functools.partial(first_kernel, dims),
        out_shape=[
            jax.ShapeDtypeStruct((ROWS, C), F32),
            jax.ShapeDtypeStruct((8, C), F32),
            *shapes_of(KEPT),
            *shapes_of(WEIGHTS),
        ],
        in_specs=[VMEM_SPEC] * 8,
        out_specs=[VMEM_SPEC] * (2 + names),
        scratch_shapes=common,
        compiler_params=PARAMS,
        name="first",
    )(flat_one, image_rows, order_first, mask_first, *consts)

    block_out, d_stream, grads_two = pl.pallas_call(
        functools.partial(second_kernel, dims),
        out_shape=[
            jax.ShapeDtypeStruct((IMG_TOK, C), F32),
            jax.ShapeDtypeStruct((ROWS, C), F32),
            grad_shape,
        ],
        in_specs=[SMEM_SPEC] + [VMEM_SPEC] * 10,
        out_specs=[VMEM_SPEC] * 3,
        scratch_shapes=scratch_of(KEPT) + scratch_of(WEIGHTS) + common + BACK_SCRATCH,
        compiler_params=PARAMS,
        name="second",
    )(counts, flat_two, stream, cot_rows, order_second, between, mask_second, *consts)

    input_grad, grads_one = pl.pallas_call(
        functools.partial(third_kernel, dims),
        out_shape=[jax.ShapeDtypeStruct((IMG_TOK, C), F32), grad_shape],
        in_specs=[SMEM_SPEC] + [VMEM_SPEC] * (7 + names),
        out_specs=[VMEM_SPEC] * 2,
        scratch_shapes=[staging] + BACK_SCRATCH,
        compiler_params=PARAMS,
        name="third",
    )(counts, d_stream, vec, order_first, *consts, *kept)

    (sum_two,) = reduce_rows([grads_two], sizes)
    (sum_one,) = reduce_rows([grads_one], sizes)
    param_grads = jnp.stack([sum_one[:shard_rows], sum_two[:shard_rows]]).astype(F32)
    param_grads = param_grads.reshape(2, shard_len)
    new_params, new_first, new_second = adam_update(params, param_grads, first_moment, second_moment)
    return (
        block_out.reshape(1, IMG_TOK, C),
        input_grad.reshape(1, IMG_TOK, C),
        param_grads,
        new_params,
        new_first,
        new_second,
    )


def solution(mesh):
    sizes = axes_of(mesh)
    axes = ("z", "y", "x", "c")
    fine = Mesh(mesh.devices.reshape(sizes), axes)
    return jax.shard_map(
        functools.partial(local, sizes),
        mesh=fine,
        in_specs=(
            P(axes, None, None),
            P(axes),
            P(axes, None, None),
            P(None, axes),
            P(None, axes),
            P(None, axes),
        ),
        out_specs=(
            P(axes, None, None),
            P(axes, None, None),
            P(None, axes),
            P(None, axes),
            P(None, axes),
            P(None, axes),
        ),
        check_vma=False,
    )
```

time: 1240 us -> 337 us (0.27); the launches traced: 1220 us -> 337 us
  local copies, waits for them, and re-layouts: 582 us -> 27.6 us
  waiting for transfers between devices: 484 us -> 192 us
  matrix products: 74 us -> 0 us
  Pallas kernels: 0 us -> 68.8 us
  other arithmetic: 58.9 us -> 18.5 us
  starting transfers between devices: 0.12 us -> 14.1 us
    unnamed x4 -> x2, waiting for transfers between devices: 389 us -> 0.71 us
    concatenate x14 -> x0, local copies, waits for them, and re-layouts: 222 us -> none  [the longest x2 198 us: pack(): return jnp.concatenate(parts_all)]
    slice x33 -> x5, local copies, waits for them, and re-layouts: 217 us -> 1.3 us  [the longest x1 0.77 us: local(): flat_one = lax.all_gather(shard[0:1], axes, axis=0, tiled=False)]
    dot_general x40 -> x0, matrix products: 74 us -> none  [the longest x2 7.22 us: layer_forward(): jnp.dot(hidden_two, weights['w_fc1'], preferred_element_type=jnp.float32)]
    ppermute x0 -> x14, waiting for transfers between devices: none -> 71.9 us  [halve(): return pick(shaped, dim + 1, low) + lax.ppermute(sent, name, pairs)]
    pallas_call x0 -> x3, Pallas kernels: none -> 68.8 us  [the longest x1 30.2 us: local(): pl.pallas_call(functools.partial(second_kernel, dims), out_shape=[jax.Sha...]
    reshape x29 -> x1, local copies, waits for them, and re-layouts: 59.4 us -> 0.67 us  [local(): shard = params.astype(BF16).reshape(2, shard_rows, LANES)]
    another operation x28 -> x0, local copies, waits for them, and re-layouts: 33.6 us -> none  [the longest x4 10.3 us: layer_backward(): to_windows(d_att.reshape(count_img, IMG_TOK, C), shifted)]
  transfers between devices with their start and end apart: 3 -> 16, of which waited for: 2 -> 11; matrix products, arithmetic and copies ran while one was open for 10% -> 7% of each run, Pallas kernels for 0% -> 5%
where the time goes in v1:
time: 337 us
  waiting for transfers between devices  192 us (57%)
  Pallas kernels  68.8 us (20%)
  local copies, waits for them, and re-layouts  27.6 us (8%)
  other arithmetic  18.5 us (5%)
  between operations  15.1 us (4%)
  starting transfers between devices  14.1 us (4%)
    ppermute x14, waiting for transfers between devices, halve(): return pick(shaped, dim + 1, low) + lax.ppermute(sent, name, pairs)  71.9 us
    all_gather x1, waiting for transfers between devices, local(): flat_one = lax.all_gather(shard[0:1], axes, axis=0, tiled=False)  67.1 us
    all_gather x1, waiting for transfers between devices, local(): flat_two = lax.all_gather(shard[1:2], axes, axis=0, tiled=False)  52.7 us
    pallas_call x1, Pallas kernels, local(): pl.pallas_call(functools.partial(second_kernel, dims), out_shape=[jax.Sha...  30.2 us
    pallas_call x1, Pallas kernels, local(): pl.pallas_call(functools.partial(third_kernel, dims), out_shape=[jax.Shap...  20.4 us
    pallas_call x1, Pallas kernels, local(): pl.pallas_call(functools.partial(first_kernel, dims), out_shape=[jax.Shap...  18.2 us
    ppermute x14, starting transfers between devices, halve(): return pick(shaped, dim + 1, low) + lax.ppermute(sent, name, pairs)  14 us
    dynamic_slice x4, local copies, waits for them, and re-layouts, pick(): return lax.dynamic_index_in_dim(values, index, axis=dim, keepdims=False)  11.1 us
  transfers between devices with their start and end apart: 16, of which 11 were waited for; matrix products, arithmetic and copies ran while one was open for 7% of the time, Pallas kernels for 5%

profile of v1, /device:TPU:0, one launch (start us, length us, event | category | flops | bytes accessed | tf_op | source)
XLA Modules:
  0.0 336.5 jit_solution(3253115622036221748)
XLA Ops:
  7.2 1.5 convert_element_type.20
  8.7 0.7 reshape.113
  9.4 0.8 pad_slice_fusion
  10.2 0.7 all-gather.5.cloned.1.call-update
  11.7 0.8 pad.12.refs_1_
  12.5 0.9 pad.13.refs_3_
  13.5 0.1 broadcast_bitcast_fusion.7
  13.6 0.1 broadcast_bitcast_fusion.8
  13.8 2.9 fusion.15.refs_7_.refs_10_
  16.7 67.1 %all-gather.7.cloned.1.call-done = bf16[32,784,128]{2,1,0:T(8,128)(2,1)} async-done(((bf16[1,784,128]{2,1,0:T(8,128)(2,1)}), bf16[32,784,128]{2,1,0:T(8,128)(2,1)}) %all-gather.7.cloned.1.call-update) | async-done | bytes 6422544 | tf_op jit(solution)/shard_map/all_gather | solution.py:594
  83.9 18.2 %first.1 = (f32[256,512]{1,0:T(8,128)}, f32[8,512]{1,0:T(8,128)}, f32[256,512]{1,0:T(8,128)}, f32[256,128]{1,0:T(8,128)}, bf16[256,512]{1,0:T(8,128)(2,1)}, /*in...) custom-call(bf16[32,1,784,128]{3,2,1,0:T(8,128)(2,1)} %bitcast.67, ...), custom_call_target="tpu_custom_call" | custom-call | tf_op jit(solution)/shard_map/first/pallas_call | solution.py:605
  102.1 52.7 %all-gather.5.cloned.1.call-done = bf16[32,784,128]{2,1,0:T(8,128)(2,1)} async-done(((bf16[1,784,128]{2,1,0:T(8,128)(2,1)}), bf16[32,784,128]{2,1,0:T(8,128)(2,1)}) %all-gather.5.cloned.1.call-update) | async-done | bytes 6422544 | tf_op jit(solution)/shard_map/all_gather | solution.py:595
  154.8 30.2 %second.1 = (f32[196,512]{1,0:T(8,128)}, f32[256,512]{1,0:T(8,128)}, bf16[32,784,128]{2,1,0:T(8,128)(2,1)}) custom-call(s32[1]{0:T(128)S(6)} %copy.54.refs_0_, bf16[32,1,784,128]{3,2,1,0:T(8,128)(2,1)} %bitcast.66, f32[256,512]{1,0:T(8,128)} %get-tuple-element.30.refs_2_, f32[256,512]{1,0:T(8,128)} %pad.13.refs_3_, ...), custom_call_target="tpu_custom_call" | custom-call | tf_op jit(solution)/shard_map/second/pallas_call | solution.py:620
  185.0 20.4 %third.1 = (f32[196,512]{1,0:T(8,128)}, bf16[32,784,128]{2,1,0:T(8,128)(2,1)}) custom-call(s32[1]{0:T(128)S(6)} %copy.54.refs_0_, f32[256,512]{1,0:T(8,128)} %get-tuple-element.32.refs_1_, f32[8,512]{1,0:T(8,128)} %get-tuple-element.33.refs_2_, bf16[256,256]{1,0:T(8,128)(2,1)} %constant.281.clone.refs_2_.refs_3_, ...), custom_call_target="tpu_custom_call" | custom-call | tf_op jit(solution)/shard_map/third/pallas_call | solution.py:634
  205.4 5.1 %constant_dynamic-slice_fusion.13 = (bf16[4,2,2,1,1,784,128]{6,5,4,2,1,0,3:T(8,128)(2,1)}, bf16[4,2,2,1,1,784,128]{6,5,4,2,1,0,3:T(8,128)(2,1)S(1)}) fusion(bf16[4,2,2,1,2,784,128]{6,5,4,2,1,0,3:T(8,128)(2,1)} %bitcast.65, s32[]{:T(128)S(6)} %select_n.166, s32[]{:T(128)S(6)} %select_n.167), kind=kLoop, calls=%fused_computation.76 | loop fusion | bytes 12845064 | tf_op jit(solution)/shard_map/jit(dynamic_index_in_dim)/dynamic_slice | solution.py:528
  210.5 2.0 copy.49
  212.5 0.3 collective-permute-start
  212.7 2.1 constant_dynamic-slice_fusion.6
  214.8 1.9 copy.48
  216.7 0.3 collective-permute-start.7
  217.0 1.4 collective-permute-done
  218.4 1.8 copy-done.7
  220.2 3.2 bitcast_add_fusion.1
  223.4 0.2 slice.34
  223.6 0.9 constant_dynamic-slice_fusion.11
  224.5 1.4 collective-permute-start.1
  226.0 0.2 copy-done.2
  226.2 2.3 bitcast_add_fusion
  228.5 1.6 copy-done
  230.1 0.1 slice.37
  230.3 1.2 copy-done.5
  231.4 0.9 constant_dynamic-slice_fusion.4
  232.4 1.4 collective-permute-start.8
  233.8 0.1 slice.35
  233.9 1.8 copy-done.1
  235.7 0.1 slice.38
  235.9 0.7 collective-permute-start.3
  236.6 1.5 collective-permute-start.10
  238.1 7.1 %collective-permute-done.1 = bf16[4,2,1,1,384,128]{5,4,0,3,2,1:T(8,128)(2,1)} collective-permute-done((bf16[4,2,1,1,384,128]{5,4,0,3,2,1:T(8,128)(2,1)}, bf16[4,2,1,1,384,128]{5,4,0,3,2,1:T(8,128)(2,1)}, u32[]{:S(2)}, u32[]{:S(2)}) %collective-permute-start.1) | collective-permute-done | bytes 786464 | tf_op jit(solution)/shard_map/ppermute | solution.py:542
  245.3 1.2 dynamic-slice_add_fusion.3
  246.6 1.6 collective-permute-start.2
  248.1 13.3 %collective-permute-done.8 = bf16[4,2,1,1,384,128]{5,4,0,3,2,1:T(8,128)(2,1)} collective-permute-done((bf16[4,2,1,1,384,128]{5,4,0,3,2,1:T(8,128)(2,1)}, bf16[4,2,1,1,384,128]{5,4,0,3,2,1:T(8,128)(2,1)}, u32[]{:S(2)}, u32[]{:S(2)}) %collective-permute-start.8) | collective-permute-done | bytes 786464 | tf_op jit(solution)/shard_map/ppermute | solution.py:542
  261.4 1.2 dynamic-slice_add_fusion.2
  262.7 1.5 collective-permute-start.9
  264.2 0.1 dynamic-slice_add_fusion.1
  264.4 0.6 collective-permute-start.4
  265.0 9.7 %collective-permute-done.10 = bf16[4,1,2,1,400,128]{5,4,0,3,2,1:T(8,128)(2,1)S(1)} collective-permute-done((bf16[4,1,2,1,400,128]{5,4,0,3,2,1:T(8,128)(2,1)S(1)}, bf16[4,1,2,1,400,128]{5,4,0,3,2,1:T(8,128)(2,1)S(1)}, u32[]{:S(2)}, u32[]{:S(2)}) %collective-permute-start.10) | collective-permute-done | bytes 819232 | tf_op jit(solution)/shard_map/ppermute | solution.py:542
  274.7 0.1 dynamic-slice_add_fusion
  274.8 0.7 collective-permute-start.11
  275.4 7.6 %collective-permute-done.2 = bf16[4,1,1,1,384,128]{5,4,0,3,2,1:T(8,128)(2,1)S(1)} collective-permute-done((bf16[4,1,1,1,384,128]{5,4,0,3,2,1:T(8,128)(2,1)S(1)}, bf16[4,1,1,1,384,128]{5,4,0,3,2,1:T(8,128)(2,1)S(1)}, u32[]{:S(2)}, u32[]{:S(2)}) %collective-permute-start.2) | collective-permute-done | bytes 393248 | tf_op jit(solution)/shard_map/ppermute | solution.py:542
  283.1 7.4 %collective-permute-done.9 = bf16[4,1,1,1,384,128]{5,4,0,3,2,1:T(8,128)(2,1)S(1)} collective-permute-done((bf16[4,1,1,1,384,128]{5,4,0,3,2,1:T(8,128)(2,1)S(1)}, bf16[4,1,1,1,384,128]{5,4,0,3,2,1:T(8,128)(2,1)S(1)}, u32[]{:S(2)}, u32[]{:S(2)}) %collective-permute-start.9) | collective-permute-done | bytes 393248 | tf_op jit(solution)/shard_map/ppermute | solution.py:542
  290.7 1.6 collective-permute-start.5
  292.5 0.8 dynamic-slice_bitcast_fusion
  293.2 0.5 collective-permute-start.12
  293.7 1.2 copy.35
  294.9 1.2 copy.34
  296.1 6.9 %collective-permute-done.5 = bf16[2,1,1,1,784,128]{5,4,3,2,1,0:T(8,128)(2,1)S(1)} collective-permute-done((bf16[2,1,1,1,784,128]{5,4,3,2,1,0:T(8,128)(2,1)S(1)}, bf16[2,1,1,1,784,128]{5,4,3,2,1,0:T(8,128)(2,1)S(1)}, u32[]{:S(2)}, u32[]{:S(2)}) %collective-permute-start.5) | collective-permute-done | bytes 401440 | tf_op jit(solution)/shard_map/ppermute | solution.py:542
  303.0 1.9 collective-permute-start.6
  304.9 9.2 %collective-permute-done.12 = bf16[2,1,1,1,784,128]{5,4,3,2,1,0:T(8,128)(2,1)} collective-permute-done((bf16[2,1,1,1,784,128]{5,4,3,2,1,0:T(8,128)(2,1)}, bf16[2,1,1,1,784,128]{5,4,3,2,1,0:T(8,128)(2,1)}, u32[]{:S(2)}, u32[]{:S(2)}) %collective-permute-start.12) | collective-permute-done | bytes 401440 | tf_op jit(solution)/shard_map/ppermute | solution.py:542
  314.1 1.0 bitcast_add_fusion.2
  315.4 0.3 copy.53
  315.7 9.2 %collective-permute-done.13 = bf16[1,1,1,1,784,128]{5,4,3,2,1,0:T(8,128)(2,1)S(1)} collective-permute-done((bf16[1,1,1,1,784,128]{5,4,3,2,1,0:T(8,128)(2,1)S(1)}, bf16[1,1,1,1,784,128]{5,4,3,2,1,0:T(8,128)(2,1)S(1)}, u32[]{:S(2)}, u32[]{:S(2)}) %collective-permute-start.13) | collective-permute-done | bytes 200736 | tf_op jit(solution)/shard_map/ppermute | solution.py:542
  324.9 0.3 copy.52
  325.3 4.4 %multiply_subtract_fusion = (f32[2,98688]{1,0:T(2,128)}, f32[2,98688]{1,0:T(2,128)}, f32[2,98688]{1,0:T(2,128)}, f32[2,98688]{1,0:T(2,128)}) fusion(f32[2,98688]{1,0:T(2,128)S(1)} %copy-done.8, f32[2,98688]{1,0:T(2,128)S(1)} %copy-done.9, f32[2,98688]{1,0:T(2,128)S(1)} %copy-done.10, bf16[1,98688]{1,0:T(2,128)(2,1)S(1)} %bitcast.75, ...), kind=kLoop, calls=%fused_computation.31 | loop fusion | flops 3750144 | bytes 5921280 | tf_op jit(solution)/shard_map/sub | solution.py:572
  (71 shorter events, 1.3 us)
Async XLA Ops:
  7.2 3.8 %copy-start.13 = (f32[1,196,512]{2,0,1:T(1,128)S(1)}, f32[1,196,512]{2,0,1:T(1,128)}, u32[]{:S(2)}) copy-start(f32[1,196,512]{2,0,1:T(1,128)} %param.14) | copy-start | bytes 1204228
  7.2 4.5 %copy-start.14 = (f32[1,196,512]{2,0,1:T(1,128)S(1)}, f32[1,196,512]{2,0,1:T(1,128)}, u32[]{:S(2)}) copy-start(f32[1,196,512]{2,0,1:T(1,128)} %param.16) | copy-start | bytes 1204228
  7.2 76.7 %all-gather.7.cloned.1.call-start = ((), (), s32[]{:S(2)}) async-start(), calls=%async_computation.1 | async-start | bytes 6623232 | tf_op jit(solution)/shard_map/all_gather | solution.py:594
  10.2 144.6 %all-gather.5.cloned.1.call-start = ((), (), s32[]{:S(2)}) async-start(), calls=%async_computation | async-start | bytes 6623232 | tf_op jit(solution)/shard_map/all_gather | solution.py:595
  205.4 7.4 %slice-start = ((s8[6422528]{0:T(1024)(128)(4,1)}), s8[4194304]{0:T(1024)(128)(4,1)S(1)}, s32[]{:S(2)}) async-start(s8[6422528]{0:T(1024)(128)(4,1)} %bitcast.62), calls=%async_computation.2 | async-start | bytes 8388608
  205.4 7.3 %slice-start.1 = ((s8[6422528]{0:T(1024)(128)(4,1)}), s8[2228224]{0:T(1024)(128)(4,1)S(1)}, s32[]{:S(2)}) async-start(s8[6422528]{0:T(1024)(128)(4,1)} %bitcast.62), calls=%async_computation.3 | async-start | bytes 4456448
  212.5 6.0 %collective-permute-start = (bf16[4,2,2,1,784,128]{5,4,0,3,2,1:T(8,128)(2,1)}, bf16[4,2,2,1,784,128]{5,4,0,3,2,1:T(8,128)(2,1)S(1)}, u32[]{:S(2)}, u32[]{:S(2)}) collective-permute-start(bf16[4,2,2,1,784,128]{5,4,0,3,2,1:T(8,128)(2,1)} %bitcast.57), channel_id=1, source_target_pairs={{0,1},{1,0},{2,3},{3,2},{4,5},{5,4},{6,7},{7,6},{8,9},{9,8},{10,11... | collective-permute-start | bytes 9633800 | tf_op jit(solution)/shard_map/ppermute | solution.py:542
  216.7 9.2 %collective-permute-start.7 = (bf16[4,2,2,1,784,128]{5,4,0,3,2,1:T(8,128)(2,1)}, bf16[4,2,2,1,784,128]{5,4,0,3,2,1:T(8,128)(2,1)}, u32[]{:S(2)}, u32[]{:S(2)}) collective-permute-start(bf16[4,2,2,1,784,128]{5,4,0,3,2,1:T(8,128)(2,1)} %bitcast.56), channel_id=1, source_target_pairs={{0,1},{1,0},{2,3},{3,2},{4,5},{5,4},{6,7},{7,6},{8,9},{9,8},{10,11... | collective-permute-start | bytes 9633800 | tf_op jit(solution)/shard_map/ppermute | solution.py:542
  218.4 1.8 copy-start.7
  223.4 2.8 copy-start.2
  223.6 2.4 copy-start.3
  224.5 20.7 %collective-permute-start.1 = (bf16[4,2,1,1,384,128]{5,4,0,3,2,1:T(8,128)(2,1)}, bf16[4,2,1,1,384,128]{5,4,0,3,2,1:T(8,128)(2,1)}, u32[]{:S(2)}, u32[]{:S(2)}) collective-permute-start(bf16[4,2,1,1,384,128]{5,4,0,3,2,1:T(8,128)(2,1)} %constant_dynamic-slice_fusion.11), channel_id=1, source_target_pairs={{0,2},{2,0},{1,3},{3,1},{4,6},{6,4},{5,7},{7,5},{8,10},{10,8},{9,1... | collective-permute-start | bytes 2359304 | tf_op jit(solution)/shard_map/ppermute | solution.py:542
  228.5 1.6 copy-start
  230.3 1.2 copy-start.5
  232.4 29.0 %collective-permute-start.8 = (bf16[4,2,1,1,384,128]{5,4,0,3,2,1:T(8,128)(2,1)}, bf16[4,2,1,1,384,128]{5,4,0,3,2,1:T(8,128)(2,1)}, u32[]{:S(2)}, u32[]{:S(2)}) collective-permute-start(bf16[4,2,1,1,384,128]{5,4,0,3,2,1:T(8,128)(2,1)} %constant_dynamic-slice_fusion.4), channel_id=1, source_target_pairs={{0,2},{2,0},{1,3},{3,1},{4,6},{6,4},{5,7},{7,5},{8,10},{10,8},{9,1... | collective-permute-start | bytes 2359304 | tf_op jit(solution)/shard_map/ppermute | solution.py:542
  233.8 1.9 copy-start.1
  235.7 9.6 %copy-start.4 = (bf16[4,2,2,1,384,128]{5,4,0,3,2,1:T(8,128)(2,1)S(1)}, bf16[4,2,2,1,384,128]{5,4,0,3,2,1:T(8,128)(2,1)}, u32[]{:S(2)}) copy-start(bf16[4,2,2,1,384,128]{5,4,0,3,2,1:T(8,128)(2,1)} %copy-done.3) | copy-start | bytes 4718596
  235.8 25.6 %copy-start.6 = (bf16[4,2,2,1,384,128]{5,4,0,3,2,1:T(8,128)(2,1)S(1)}, bf16[4,2,2,1,384,128]{5,4,0,3,2,1:T(8,128)(2,1)}, u32[]{:S(2)}) copy-start(bf16[4,2,2,1,384,128]{5,4,0,3,2,1:T(8,128)(2,1)} %copy-done.5) | copy-start | bytes 4718596
  235.9 28.3 %collective-permute-start.3 = (bf16[4,1,2,1,400,128]{5,4,0,3,2,1:T(8,128)(2,1)S(1)}, bf16[4,1,2,1,400,128]{5,4,0,3,2,1:T(8,128)(2,1)S(1)}, u32[]{:S(2)}, u32[]{:S(2)}) collective-permute-start(bf16[4,1,2,1,400,128]{5,4,0,3,2,1:T(8,128)(2,1)S(1)} %constant_dynamic-slice_fusion.9), channel_id=1, source_target_pairs={{0,4},{4,0},{1,5},{5,1},{2,6},{6,2},{3,7},{7,3},{8,12},{12,8},{9,1... | collective-permute-start | bytes 2457608 | tf_op jit(solution)/shard_map/ppermute | solution.py:542
  236.6 38.0 %collective-permute-start.10 = (bf16[4,1,2,1,400,128]{5,4,0,3,2,1:T(8,128)(2,1)S(1)}, bf16[4,1,2,1,400,128]{5,4,0,3,2,1:T(8,128)(2,1)S(1)}, u32[]{:S(2)}, u32[]{:S(2)}) collective-permute-start(bf16[4,1,2,1,400,128]{5,4,0,3,2,1:T(8,128)(2,1)S(1)} %constant_dynamic-slice_fusion.2), channel_id=1, source_target_pairs={{0,4},{4,0},{1,5},{5,1},{2,6},{6,2},{3,7},{7,3},{8,12},{12,8},{9,1... | collective-permute-start | bytes 2457608 | tf_op jit(solution)/shard_map/ppermute | solution.py:542
  246.6 36.5 %collective-permute-start.2 = (bf16[4,1,1,1,384,128]{5,4,0,3,2,1:T(8,128)(2,1)S(1)}, bf16[4,1,1,1,384,128]{5,4,0,3,2,1:T(8,128)(2,1)S(1)}, u32[]{:S(2)}, u32[]{:S(2)}) collective-permute-start(bf16[4,1,1,1,384,128]{5,4,0,3,2,1:T(8,128)(2,1)S(1)} %constant_dynamic-slice_fusion.10), channel_id=1, source_target_pairs={{0,4},{4,0},{1,5},{5,1},{2,6},{6,2},{3,7},{7,3},{8,12},{12,8},{9,1... | collective-permute-start | bytes 1179656 | tf_op jit(solution)/shard_map/ppermute | solution.py:542
  262.7 27.8 %collective-permute-start.9 = (bf16[4,1,1,1,384,128]{5,4,0,3,2,1:T(8,128)(2,1)S(1)}, bf16[4,1,1,1,384,128]{5,4,0,3,2,1:T(8,128)(2,1)S(1)}, u32[]{:S(2)}, u32[]{:S(2)}) collective-permute-start(bf16[4,1,1,1,384,128]{5,4,0,3,2,1:T(8,128)(2,1)S(1)} %constant_dynamic-slice_fusion.3), channel_id=1, source_target_pairs={{0,4},{4,0},{1,5},{5,1},{2,6},{6,2},{3,7},{7,3},{8,12},{12,8},{9,1... | collective-permute-start | bytes 1179656 | tf_op jit(solution)/shard_map/ppermute | solution.py:542
  264.4 26.2 %collective-permute-start.4 = (bf16[4,1,1,1,400,128]{5,4,0,3,2,1:T(8,128)(2,1)S(1)}, bf16[4,1,1,1,400,128]{5,4,0,3,2,1:T(8,128)(2,1)S(1)}, u32[]{:S(2)}, u32[]{:S(2)}) collective-permute-start(bf16[4,1,1,1,400,128]{5,4,0,3,2,1:T(8,128)(2,1)S(1)} %constant_dynamic-slice_fusion.8), channel_id=1, source_target_pairs={{0,2},{2,0},{1,3},{3,1},{4,6},{6,4},{5,7},{7,5},{8,10},{10,8},{9,1... | collective-permute-start | bytes 1228808 | tf_op jit(solution)/shard_map/ppermute | solution.py:542
  274.8 17.6 %collective-permute-start.11 = (bf16[4,1,1,1,400,128]{5,4,0,3,2,1:T(8,128)(2,1)S(1)}, bf16[4,1,1,1,400,128]{5,4,0,3,2,1:T(8,128)(2,1)S(1)}, u32[]{:S(2)}, u32[]{:S(2)}) collective-permute-start(bf16[4,1,1,1,400,128]{5,4,0,3,2,1:T(8,128)(2,1)S(1)} %constant_dynamic-slice_fusion.1), channel_id=1, source_target_pairs={{0,2},{2,0},{1,3},{3,1},{4,6},{6,4},{5,7},{7,5},{8,10},{10,8},{9,1... | collective-permute-start | bytes 1228808 | tf_op jit(solution)/shard_map/ppermute | solution.py:542
  290.6 3.1 copy-start.12
  290.6 4.3 %copy-start.11 = (f32[196,512]{1,0:T(8,128)S(1)}, f32[196,512]{1,0:T(8,128)}, u32[]{:S(2)}) copy-start(f32[196,512]{1,0:T(8,128)} %get-tuple-element.31) | copy-start | bytes 1204228
  290.7 12.2 %collective-permute-start.5 = (bf16[2,1,1,1,784,128]{5,4,3,2,1,0:T(8,128)(2,1)S(1)}, bf16[2,1,1,1,784,128]{5,4,3,2,1,0:T(8,128)(2,1)S(1)}, u32[]{:S(2)}, u32[]{:S(2)}) collective-permute-start(bf16[2,1,1,1,784,128]{5,4,3,2,1,0:T(8,128)(2,1)S(1)} %dynamic-slice_bitcast_fusion.1), channel_id=1, source_target_pairs={{0,8},{8,0},{16,24},{24,16},{1,9},{9,1},{17,25},{25,17},{2,10},{10... | collective-permute-start | bytes 1204232 | tf_op jit(solution)/shard_map/ppermute | solution.py:542
  293.2 20.9 %collective-permute-start.12 = (bf16[2,1,1,1,784,128]{5,4,3,2,1,0:T(8,128)(2,1)}, bf16[2,1,1,1,784,128]{5,4,3,2,1,0:T(8,128)(2,1)}, u32[]{:S(2)}, u32[]{:S(2)}) collective-permute-start(bf16[2,1,1,1,784,128]{5,4,3,2,1,0:T(8,128)(2,1)} %dynamic-slice_bitcast_fusion), channel_id=1, source_target_pairs={{0,8},{8,0},{16,24},{24,16},{1,9},{9,1},{17,25},{25,17},{2,10},{10... | collective-permute-start | bytes 1204232 | tf_op jit(solution)/shard_map/ppermute | solution.py:542
  294.9 30.3 %copy-start.8 = (f32[2,98688]{1,0:T(2,128)S(1)}, f32[2,98688]{1,0:T(2,128)}, u32[]{:S(2)}) copy-start(f32[2,98688]{1,0:T(2,128)} %param.17) | copy-start | bytes 2368516
  294.9 30.3 %copy-start.9 = (f32[2,98688]{1,0:T(2,128)S(1)}, f32[2,98688]{1,0:T(2,128)}, u32[]{:S(2)}) copy-start(f32[2,98688]{1,0:T(2,128)} %param.18) | copy-start | bytes 2368516
  294.9 30.3 %copy-start.10 = (f32[2,98688]{1,0:T(2,128)S(1)}, f32[2,98688]{1,0:T(2,128)}, u32[]{:S(2)}) copy-start(f32[2,98688]{1,0:T(2,128)} %param.19) | copy-start | bytes 2368516
  303.0 12.2 %collective-permute-start.6 = (bf16[1,1,1,1,784,128]{5,4,3,2,1,0:T(8,128)(2,1)S(1)}, bf16[1,1,1,1,784,128]{5,4,3,2,1,0:T(8,128)(2,1)S(1)}, u32[]{:S(2)}, u32[]{:S(2)}) collective-permute-start(bf16[1,1,1,1,784,128]{5,4,3,2,1,0:T(8,128)(2,1)S(1)} %constant_dynamic-slice_fusion.7), channel_id=1, source_target_pairs={{0,16},{8,24},{16,0},{24,8},{1,17},{9,25},{17,1},{25,9},{2,18},{10... | collective-permute-start | bytes 602120 | tf_op jit(solution)/shard_map/ppermute | solution.py:542
  315.2 9.7 %collective-permute-start.13 = (bf16[1,1,1,1,784,128]{5,4,3,2,1,0:T(8,128)(2,1)S(1)}, bf16[1,1,1,1,784,128]{5,4,3,2,1,0:T(8,128)(2,1)S(1)}, u32[]{:S(2)}, u32[]{:S(2)}) collective-permute-start(bf16[1,1,1,1,784,128]{5,4,3,2,1,0:T(8,128)(2,1)S(1)} %constant_dynamic-slice_fusion), channel_id=1, source_target_pairs={{0,16},{8,24},{16,0},{24,8},{1,17},{9,25},{17,1},{25,9},{2,18},{10... | collective-permute-start | bytes 602120 | tf_op jit(solution)/shard_map/ppermute | solution.py:542
Sparse Core Ops, SparseCore 0:
  11.4 72.3 all-gather.6
  86.7 68.0 all-gather.4

commit v2 on v1

--- a/solution.py
+++ b/solution.py
@@ -130,32 +130,50 @@
     return dot(onehot, high) + dot(onehot, middle) + dot(onehot, low)
 
 
-def flat_to_staging(flat_ref, block, staging, device_count, shard_rows):
+def fetch_pieces(pieces, buffer, sems, sizes, cut):
+    z, y, x, _ = sizes
+    view = buffer.reshape((z, y, x, 2) + buffer.shape[1:])
+    copies = []
+    at = 0
+    for core in range(2):
+        for part in range(2):
+            rows = slice(0, cut) if part == 0 else slice(cut, buffer.shape[1])
+            for late in range(2):
+                piece = pieces[at]
+                at += 1
+                for i in range(piece.shape[1]):
+                    for j in range(piece.shape[2]):
+                        yy, xx = (i + late * piece.shape[1], j) if part == 0 else (i, j + late * piece.shape[2])
+                        copies.append(
+                            pltpu.make_async_copy(
+                                piece.at[:, i, j], view.at[:, yy, xx, core, rows, :], sems.at[len(copies)]
+                            )
+                        )
+    for copy in copies:
+        copy.start()
+    for copy in copies:
+        copy.wait()
+
+
+def flat_to_staging(buffer, staging, place, device_count, shard_rows):
     group = 8
 
     @pl.loop(0, device_count // group)
     def _(step):
         view = staging.at[pl.ds(pl.multiple_of(step * group * shard_rows, 8), group * shard_rows), :]
         for i in range(group):
-            view[i * shard_rows : (i + 1) * shard_rows, :] = flat_ref[
-                step * group + i, block, :shard_rows, :
-            ].astype(F32)
-
-
-def staging_to_flat(staging, flat_ref, device_count, shard_rows, padded_rows):
-    group = 8
-
-    @pl.loop(0, device_count // group)
-    def _(step):
-        view = staging.at[pl.ds(pl.multiple_of(step * group * shard_rows, 8), group * shard_rows), :]
-        for i in range(group):
-            flat_ref[step * group + i, :shard_rows, :] = view[
-                i * shard_rows : (i + 1) * shard_rows, :
-            ].astype(BF16)
+            slot = lax.bitwise_xor(step * group + i, place)
+            view[i * shard_rows : (i + 1) * shard_rows, :] = buffer[slot, :shard_rows, :].astype(F32)
+
+
+def staging_to_flat(staging, keep_ref, send_ref, place, device_count, shard_rows, padded_rows):
+    @pl.loop(0, device_count // 2)
+    def _(pair):
+        for core, target in enumerate((keep_ref, send_ref)):
+            owner = lax.bitwise_xor(pair * 2 + core, place)
+            target[pair, :shard_rows, :] = staging[pl.ds(owner * shard_rows, shard_rows), :].astype(BF16)
             if padded_rows > shard_rows:
-                flat_ref[step * group + i, shard_rows:, :] = jnp.zeros(
-                    (padded_rows - shard_rows, LANES), BF16
-                )
+                target[pair, shard_rows:, :] = jnp.zeros((padded_rows - shard_rows, LANES), BF16)
 
 
 def unpack_matrix(staging, target, base, pitch, chunk):
@@ -437,22 +455,24 @@
 ]
 
 
-def unpack_weights(flat_ref, block, staging, w, device_count, shard_rows):
-    flat_to_staging(flat_ref, block, staging, device_count, shard_rows)
+def unpack_weights(pieces, buffer, sems, staging, w, place, dims):
+    sizes, shard_rows, padded_rows, cut = dims
+    fetch_pieces(pieces, buffer, sems, sizes, cut)
+    flat_to_staging(buffer, staging, place, math.prod(sizes), shard_rows)
     unpack_matrix(staging, w["qkv"], BASE_QKV, PITCH_QKV, 128)
     unpack_matrix(staging, w["out"], BASE_OUT, PITCH_OUT, 128)
     unpack_matrix(staging, w["fc1"], BASE_FC1, PITCH_FC1, 128)
     unpack_matrix(staging, w["fc2"], BASE_FC2, PITCH_FC2, 256)
 
 
-def first_kernel(sizes, *refs):
-    device_count, shard_rows, padded_rows = sizes
-    flat, images, order, mask, rows_c, lane_c, heads_c, offsets = refs[:8]
+def first_kernel(dims, *refs):
+    place, *pieces = refs[:9]
+    images, order, mask, rows_c, lane_c, heads_c, offsets = refs[9:16]
     names = list(KEPT) + list(WEIGHTS)
-    stream, vec_out, *outs = refs[8 : 10 + len(names)]
-    staging, shift, bias = refs[10 + len(names) :]
+    stream, vec_out, *outs = refs[16 : 18 + len(names)]
+    staging, shift, bias, buffer, sems = refs[18 + len(names) :]
     kept = dict(zip(names, outs))
-    unpack_weights(flat, 0, staging, kept, device_count, shard_rows)
+    unpack_weights(pieces, buffer, sems, staging, kept, place[0], dims)
     vec, b_fc1 = unpack_tail(staging, shift, None)
     vec_out[...] = jnp.concatenate(vec, axis=0)
     build_bias(staging, rows_c, lane_c, heads_c, offsets, bias)
@@ -460,14 +480,16 @@
     stream[...] = block_forward(x, kept, vec, b_fc1, bias, mask, kept)
 
 
-def second_kernel(sizes, *refs):
-    device_count, shard_rows, padded_rows = sizes
-    valid, flat, stream, cotangent, order, between, mask, rows_c, lane_c, heads_c, offsets = refs[:11]
-    block_out, d_stream, grads = refs[11:14]
+def second_kernel(dims, *refs):
+    sizes, shard_rows, padded_rows, _ = dims
+    device_count = math.prod(sizes)
+    valid, place, *pieces = refs[:10]
+    stream, cotangent, order, between, mask, rows_c, lane_c, heads_c, offsets = refs[10:19]
+    block_out, d_stream, keep, send = refs[19:23]
     names = list(KEPT) + list(WEIGHTS)
-    kept = dict(zip(names, refs[14 : 14 + len(names)]))
-    staging, shift, bias, *scratch = refs[14 + len(names) :]
-    unpack_weights(flat, 0, staging, kept, device_count, shard_rows)
+    kept = dict(zip(names, refs[23 : 23 + len(names)]))
+    staging, shift, bias, buffer, sems, *scratch = refs[23 + len(names) :]
+    unpack_weights(pieces, buffer, sems, staging, kept, place[0], dims)
     vec, b_fc1 = unpack_tail(staging, shift, None)
     build_bias(staging, rows_c, lane_c, heads_c, offsets, bias)
     factor = (valid[0] > 0).astype(F32)
@@ -481,25 +503,27 @@
         device_count, shard_rows,
     )
     d_stream[...] = select_rows(between[...].T, d_in)
-    staging_to_flat(staging, grads, device_count, shard_rows, padded_rows)
-
-
-def third_kernel(sizes, *refs):
-    device_count, shard_rows, padded_rows = sizes
-    valid, d_stream, vec, order, rows_c, lane_c, heads_c, offsets = refs[:8]
+    staging_to_flat(staging, keep, send, place[0], device_count, shard_rows, padded_rows)
+
+
+def third_kernel(dims, *refs):
+    sizes, shard_rows, padded_rows, _ = dims
+    device_count = math.prod(sizes)
+    valid, place, d_stream, vec, order, rows_c, lane_c, heads_c, offsets = refs[:9]
     names = list(KEPT) + list(WEIGHTS)
-    kept = dict(zip(names, refs[8 : 8 + len(names)]))
-    input_grad, grads = refs[8 + len(names) : 10 + len(names)]
-    staging, *scratch = refs[10 + len(names) :]
+    kept = dict(zip(names, refs[9 : 9 + len(names)]))
+    input_grad, keep, send = refs[9 + len(names) : 12 + len(names)]
+    staging, *scratch = refs[12 + len(names) :]
     factor = (valid[0] > 0).astype(F32)
     d_in = block_backward(
         d_stream[...], kept, vec[0:1, :], vec[5:6, :], kept, staging,
         (rows_c, lane_c, heads_c, offsets), scratch, device_count, shard_rows,
     )
     input_grad[...] = select_rows(order[...].T, d_in)[:IMG_TOK] * factor
-    staging_to_flat(staging, grads, device_count, shard_rows, padded_rows)
-
-
+    staging_to_flat(staging, keep, send, place[0], device_count, shard_rows, padded_rows)
+
+
+ANY_SPEC = pl.BlockSpec(memory_space=pl.ANY)
 VMEM_SPEC = pl.BlockSpec(memory_space=pltpu.VMEM)
 SMEM_SPEC = pl.BlockSpec(memory_space=pltpu.SMEM)
 PARAMS = pltpu.CompilerParams(vmem_limit_bytes=60 * 1024 * 1024)
@@ -520,47 +544,73 @@
     return int(extent[2]), int(extent[1]), int(extent[0]), int(extent[3])
 
 
-def flip(values, axis):
-    return lax.ppermute(values, axis, [(0, 1), (1, 0)])
-
-
-def pick(values, dim, index):
-    return lax.dynamic_index_in_dim(values, index, axis=dim, keepdims=False)
-
-
-def reduce_rows(grads, sizes):
-    names = ("z", "y", "x", "c")
-    parts = [g.reshape(tuple(sizes) + g.shape[1:]) for g in grads]
-    def halve(values, dim, name, size, bit):
-        place = lax.axis_index(name)
-        step = 1 << bit
-        low = (place // step) % 2
-        span = values.shape[dim]
-        shaped = values.reshape(values.shape[:dim] + (span // 2, 2) + values.shape[dim + 1 :])
-        sent = pick(shaped, dim + 1, 1 - low)
-        pairs = [(i, i ^ step) for i in range(size)]
-        return pick(shaped, dim + 1, low) + lax.ppermute(sent, name, pairs)
-
-    def along(values, dim, name, size):
-        bit = 0
-        while (1 << bit) < size:
-            values = halve(values, dim, name, size, bit)
-            bit += 1
-        return values
-
-    z, y, x, c = sizes
-    parts = [along(p, 3, "c", c) for p in parts]
-    rows = parts[0].shape[4]
-    cut = rows // 2 // 16 * 16
-    first = [p[..., :cut, :] for p in parts]
-    second = [p[..., cut:, :] for p in parts]
-    first = [along(p, 2, "x", x) for p in first]
-    second = [along(p, 1, "y", y) for p in second]
-    first = [along(p, 1, "y", y) for p in first]
-    second = [along(p, 2, "x", x) for p in second]
-    parts = [jnp.concatenate([a, b], axis=4) for a, b in zip(first, second)]
-    parts = [along(p, 0, "z", z) for p in parts]
-    return [p.reshape(p.shape[4:]) for p in parts]
+AXES = ("z", "y", "x", "c")
+
+
+def swap(values, axis, size, step):
+    return lax.ppermute(values, axis, [(i, i ^ step) for i in range(size)])
+
+
+def bits_of(size):
+    return [1 << b for b in range(size.bit_length() - 1)]
+
+
+def after(values, *others):
+    return lax.optimization_barrier((values,) + others)[0]
+
+
+class Gather:
+    def __init__(self, shard, sizes, cut):
+        self.sizes, self.cut = sizes, cut
+        self.whole = shard.reshape((1, 1, 1) + shard.shape)
+
+    def grow(self, values, name, step):
+        dim = AXES.index(name)
+        got = swap(values, name, self.sizes[dim], step)
+        count = values.shape[dim]
+        shape = values.shape[:dim] + (count, 1) + values.shape[dim + 1 :]
+        joined = jnp.concatenate([values.reshape(shape), got.reshape(shape)], axis=dim + 1)
+        return joined.reshape(values.shape[:dim] + (count * 2,) + values.shape[dim + 1 :]), got
+
+    def along_z(self, gate=None):
+        for at, step in enumerate(reversed(bits_of(self.sizes[0]))):
+            if gate is not None and at < len(gate):
+                self.whole = after(self.whole, gate[at])
+            self.whole, got = self.grow(self.whole, "z", step)
+            yield got
+
+    def split(self):
+        self.first = self.whole[..., : self.cut, :]
+        self.second = self.whole[..., self.cut :, :]
+
+    def across(self):
+        z, y, x, c = self.sizes
+        for step in reversed(bits_of(x)):
+            self.first, got_first = self.grow(self.first, "x", step)
+        for step in reversed(bits_of(y)):
+            self.second, got_second = self.grow(self.second, "y", step)
+        for step in reversed(bits_of(y)[1:]):
+            self.first, got_first = self.grow(self.first, "y", step)
+        for step in reversed(bits_of(x)[1:]):
+            self.second, got_second = self.grow(self.second, "x", step)
+        return got_first, got_second
+
+    def last(self):
+        z, y, x, c = self.sizes
+        return swap(self.first, "y", y, 1), swap(self.second, "x", x, 1)
+
+
+def reduce_core(keep, sent, sizes):
+    return keep, swap(sent, "c", sizes[3], 1)
+
+
+def shed(values, got, dim, name, size, step):
+    total = values if got is None else values + got
+    span = total.shape[dim]
+    shaped = total.reshape(total.shape[:dim] + (span // 2, 2) + total.shape[dim + 1 :])
+    mine = lax.index_in_dim(shaped, 0, dim + 1, keepdims=False)
+    theirs = lax.index_in_dim(shaped, 1, dim + 1, keepdims=False)
+    return mine, swap(theirs, name, size, step)
 
 
 def adam_update(weights_now, grads_now, moment_one, moment_two):
@@ -577,7 +627,6 @@
     shard_len = params.shape[1]
     shard_rows = shard_len // LANES
     padded_rows = round_up(shard_rows, 16)
-    dims = (device_count, shard_rows, padded_rows)
     flat_rows = device_count * shard_rows
 
     take_first, take_second = order_matrices()
@@ -588,20 +637,50 @@
     mask_first, mask_second = jnp.asarray(masks[0]), jnp.asarray(masks[1])
     consts = [jnp.asarray(a, BF16) for a in table_constants()] + [offset_lanes()]
 
+    cut = padded_rows // 2 // 16 * 16
+    dims = (sizes, shard_rows, padded_rows, cut)
+    place = lax.axis_index(AXES).astype(jnp.int32).reshape(1)
+
     shard = params.astype(BF16).reshape(2, shard_rows, LANES)
     shard = jnp.pad(shard, ((0, 0), (0, padded_rows - shard_rows), (0, 0)))
-    axes = ("z", "y", "x", "c")
-    flat_one = lax.all_gather(shard[0:1], axes, axis=0, tiled=False)
-    flat_two = lax.all_gather(shard[1:2], axes, axis=0, tiled=False)
+    one, two = Gather(shard[0], sizes, cut), Gather(shard[1], sizes, cut)
+    gates = []
+    for got in one.along_z():
+        gates.append(got)
+    two.whole = after(two.whole, gates[-1])
+    one.split()
+    across_one = one.across()
+    steps_two = two.along_z([gates[-1], across_one[0]])
+    for _ in steps_two:
+        pass
+    two.split()
+    last_one = one.last()
+    early_one = (swap(one.first, "c", 2, 1), swap(one.second, "c", 2, 1))
+    late_one = tuple(swap(v, "c", 2, 1) for v in last_one)
+    pieces_one = [one.first, last_one[0], one.second, last_one[1], early_one[0], late_one[0], early_one[1], late_one[1]]
+    two.first = after(two.first, last_one[0])
+    two.second = after(two.second, last_one[1])
+    two.across()
+    last_two = two.last()
+    early_two = (swap(two.first, "c", 2, 1), swap(two.second, "c", 2, 1))
+    late_two = tuple(swap(v, "c", 2, 1) for v in last_two)
+    pieces_two = [two.first, last_two[0], two.second, last_two[1], early_two[0], late_two[0], early_two[1], late_two[1]]
 
     pad_tokens = ((0, ROWS - IMG_TOK), (0, 0))
     image_rows = jnp.pad(images.reshape(IMG_TOK, C), pad_tokens)
     cot_rows = jnp.pad(cotangent.reshape(IMG_TOK, C), pad_tokens)
 
-    grad_shape = jax.ShapeDtypeStruct((device_count, padded_rows, LANES), BF16)
+    half_shape = jax.ShapeDtypeStruct((device_count // 2, padded_rows, LANES), BF16)
     names = len(KEPT) + len(WEIGHTS)
     staging = pltpu.VMEM((flat_rows, LANES), F32)
-    common = [staging, pltpu.VMEM((96, LANES), F32), pltpu.VMEM((512, LANES), F32)]
+    copy_count = 2 * sum(math.prod(p.shape[1:3]) for p in pieces_one[:4])
+    common = [
+        staging,
+        pltpu.VMEM((96, LANES), F32),
+        pltpu.VMEM((512, LANES), F32),
+        pltpu.VMEM((device_count, padded_rows, LANES), BF16),
+        pltpu.SemaphoreType.DMA((copy_count,)),
+    ]
     stream, vec, *kept = pl.pallas_call(
         functools.partial(first_kernel, dims),
         out_shape=[
@@ -610,40 +689,68 @@
             *shapes_of(KEPT),
             *shapes_of(WEIGHTS),
         ],
-        in_specs=[VMEM_SPEC] * 8,
+        in_specs=[SMEM_SPEC] + [ANY_SPEC] * 8 + [VMEM_SPEC] * 7,
         out_specs=[VMEM_SPEC] * (2 + names),
         scratch_shapes=common,
         compiler_params=PARAMS,
         name="first",
-    )(flat_one, image_rows, order_first, mask_first, *consts)
-
-    block_out, d_stream, grads_two = pl.pallas_call(
+    )(place, *pieces_one, image_rows, order_first, mask_first, *consts)
+
+    block_out, d_stream, keep_two, send_two = pl.pallas_call(
         functools.partial(second_kernel, dims),
         out_shape=[
             jax.ShapeDtypeStruct((IMG_TOK, C), F32),
             jax.ShapeDtypeStruct((ROWS, C), F32),
-            grad_shape,
+            half_shape,
+            half_shape,
         ],
-        in_specs=[SMEM_SPEC] + [VMEM_SPEC] * 10,
-        out_specs=[VMEM_SPEC] * 3,
+        in_specs=[SMEM_SPEC] * 2 + [ANY_SPEC] * 8 + [VMEM_SPEC] * 9,
+        out_specs=[VMEM_SPEC] * 4,
         scratch_shapes=scratch_of(KEPT) + scratch_of(WEIGHTS) + common + BACK_SCRATCH,
         compiler_params=PARAMS,
         name="second",
-    )(counts, flat_two, stream, cot_rows, order_second, between, mask_second, *consts)
-
-    input_grad, grads_one = pl.pallas_call(
+    )(counts, place, *pieces_two, stream, cot_rows, order_second, between, mask_second, *consts)
+
+    z, y, x, c = sizes
+
+    def begin(keep, sent):
+        got = swap(sent, "c", c, 1)
+        shape = (z, y, x, padded_rows, LANES)
+        keep, got = keep.reshape(shape), got.reshape(shape)
+        top = shed(keep[..., :cut, :], got[..., :cut, :], 2, "x", x, 1)
+        low = shed(keep[..., cut:, :], got[..., cut:, :], 1, "y", y, 1)
+        return top, low
+
+    def finish(top, low):
+        for step in bits_of(x)[1:]:
+            top = shed(*top, 2, "x", x, step)
+        for step in bits_of(y)[1:]:
+            low = shed(*low, 1, "y", y, step)
+        for step in bits_of(y):
+            top = shed(*top, 1, "y", y, step)
+        for step in bits_of(x):
+            low = shed(*low, 2, "x", x, step)
+        both = tuple(jnp.concatenate([a, b], axis=3) for a, b in zip(top, low))
+        for step in bits_of(z):
+            both = shed(*both, 0, "z", z, step)
+        mine, got = both
+        return (mine.astype(F32) + got.astype(F32)).reshape(padded_rows, LANES)
+
+    top_two, low_two = begin(keep_two, send_two)
+    d_stream = after(d_stream, top_two[0], low_two[0])
+    input_grad, keep_one, send_one = pl.pallas_call(
         functools.partial(third_kernel, dims),
-        out_shape=[jax.ShapeDtypeStruct((IMG_TOK, C), F32), grad_shape],
-        in_specs=[SMEM_SPEC] + [VMEM_SPEC] * (7 + names),
-        out_specs=[VMEM_SPEC] * 2,
+        out_shape=[jax.ShapeDtypeStruct((IMG_TOK, C), F32), half_shape, half_shape],
+        in_specs=[SMEM_SPEC] * 2 + [VMEM_SPEC] * (7 + names),
+        out_specs=[VMEM_SPEC] * 3,
         scratch_shapes=[staging] + BACK_SCRATCH,
         compiler_params=PARAMS,
         name="third",
-    )(counts, d_stream, vec, order_first, *consts, *kept)
-
-    (sum_two,) = reduce_rows([grads_two], sizes)
-    (sum_one,) = reduce_rows([grads_one], sizes)
-    param_grads = jnp.stack([sum_one[:shard_rows], sum_two[:shard_rows]]).astype(F32)
+    )(counts, place, d_stream, vec, order_first, *consts, *kept)
+    top_one, low_one = begin(keep_one, send_one)
+    sum_two = finish(top_two, low_two)
+    sum_one = finish(top_one, low_one)
+    param_grads = jnp.stack([sum_one[:shard_rows], sum_two[:shard_rows]])
     param_grads = param_grads.reshape(2, shard_len)
     new_params, new_first, new_second = adam_update(params, param_grads, first_moment, second_moment)
     return (
@@ -658,7 +765,7 @@
 
 def solution(mesh):
     sizes = axes_of(mesh)
-    axes = ("z", "y", "x", "c")
+    axes = AXES
     fine = Mesh(mesh.devices.reshape(sizes), axes)
     return jax.shard_map(
         functools.partial(local, sizes),

time: 337 us -> 274 us (0.81); the launches traced: 337 us -> 270 us
  waiting for transfers between devices: 192 us -> 119 us
  starting transfers between devices: 14.1 us -> 45.2 us
  between operations: 15.1 us -> 2.08 us
  local copies, waits for them, and re-layouts: 27.6 us -> 19.8 us
  other arithmetic: 18.5 us -> 14.1 us
    all_gather x2 -> x0, waiting for transfers between devices: 120 us -> none  [the longest x1 67.1 us: local(): flat_one = lax.all_gather(shard[0:1], axes, axis=0, tiled=False)]
    ppermute x14 -> x34, waiting for transfers between devices: 71.9 us -> 119 us  [swap(): return lax.ppermute(values, axis, [(i, i ^ step) for i in range(size)])]
    ppermute x14 -> x34, starting transfers between devices: 14 us -> 45.2 us  [swap(): return lax.ppermute(values, axis, [(i, i ^ step) for i in range(size)])]
    dynamic_slice x4 -> x0, local copies, waits for them, and re-layouts: 11.1 us -> none  [pick(): return lax.dynamic_index_in_dim(values, index, axis=dim, keepdims=False)]
    ppermute x0 -> x6, local copies, waits for them, and re-layouts: none -> 9.01 us  [swap(): return lax.ppermute(values, axis, [(i, i ^ step) for i in range(size)])]
    add x12 -> x2, other arithmetic: 9.4 us -> 0.42 us  [shed(): total = values if got is None else values + got]
    unnamed x40 -> x38, local copies, waits for them, and re-layouts: 9.57 us -> 5.29 us
    reshape x0 -> x15, other arithmetic: none -> 4.16 us  [the longest x10 3.83 us: shed(): total.reshape(total.shape[:dim] + (span // 2, 2) + total.shape[dim + 1:])]
  transfers between devices with their start and end apart: 16 -> 34, of which waited for: 11 -> 19; matrix products, arithmetic and copies ran while one was open for 7% -> 10% of each run, Pallas kernels for 5% -> 7%
where the time goes in v2:
time: 274 us; the launch traced here: 270 us
  waiting for transfers between devices  119 us (43%)
  Pallas kernels  70.2 us (26%)
  starting transfers between devices  45.2 us (16%)
  local copies, waits for them, and re-layouts  19.8 us (7%)
  other arithmetic  14.1 us (5%)
    ppermute x34, waiting for transfers between devices, swap(): return lax.ppermute(values, axis, [(i, i ^ step) for i in range(size)])  119 us
    ppermute x34, starting transfers between devices, swap(): return lax.ppermute(values, axis, [(i, i ^ step) for i in range(size)])  45.2 us
    pallas_call x1, Pallas kernels, local(): pl.pallas_call(functools.partial(second_kernel, dims), out_shape=[jax.Sha...  31.4 us
    pallas_call x1, Pallas kernels, local(): pl.pallas_call(functools.partial(third_kernel, dims), out_shape=[jax.Shap...  20.7 us
    pallas_call x1, Pallas kernels, local(): pl.pallas_call(functools.partial(first_kernel, dims), out_shape=[jax.Shap...  18.2 us
    ppermute x6, local copies, waits for them, and re-layouts, swap(): return lax.ppermute(values, axis, [(i, i ^ step) for i in range(size)])  9.01 us
  transfers between devices with their start and end apart: 34, of which 19 were waited for; matrix products, arithmetic and copies ran while one was open for 10% of the time, Pallas kernels for 7%

profile of v2, /device:TPU:0, one launch (start us, length us, event | category | flops | bytes accessed | tf_op | source)
XLA Modules:
  0.0 270.1 jit_solution(16768253273630701401)
XLA Ops:
  0.6 1.4 convert_element_type.50
  2.0 0.7 reshape.347
  2.8 4.1 %collective-permute-start = (bf16[1,1,1,784,128]{4,3,2,1,0:T(8,128)(2,1)S(1)}, bf16[1,1,1,784,128]{4,3,2,1,0:T(8,128)(2,1)S(1)}, u32[]{:S(2)}, u32[]{:S(2)}) collective-permute-start(bf16[1,1,1,784,128]{4,3,2,1,0:T(8,128)(2,1)S(1)} %get-tuple-element.111), channel_id=1, source_target_pairs={{0,16},{8,24},{16,0},{24,8},{1,17},{9,25},{17,1},{25,9},{2,18},{10... | collective-permute-start | bytes 602120 | tf_op jit(solution)/shard_map/ppermute | solution.py:551
  6.9 9.3 %collective-permute-done = bf16[1,1,1,784,128]{4,3,2,1,0:T(8,128)(2,1)S(1)} collective-permute-done((bf16[1,1,1,784,128]{4,3,2,1,0:T(8,128)(2,1)S(1)}, bf16[1,1,1,784,128]{4,3,2,1,0:T(8,128)(2,1)S(1)}, u32[]{:S(2)}, u32[]{:S(2)}) %collective-permute-start) | collective-permute-done | bytes 200736 | tf_op jit(solution)/shard_map/ppermute | solution.py:551
  16.3 0.8 collective-permute-start.1
  17.1 9.7 %collective-permute-done.1 = bf16[2,1,1,784,128]{4,3,0,2,1:T(8,128)(2,1)S(1)} collective-permute-done((bf16[2,1,1,784,128]{4,3,0,2,1:T(8,128)(2,1)S(1)}, bf16[2,1,1,784,128]{4,3,0,2,1:T(8,128)(2,1)S(1)}, u32[]{:S(2)}, u32[]{:S(2)}) %collective-permute-start.1) | collective-permute-done | bytes 401440 | tf_op jit(solution)/shard_map/ppermute | solution.py:551
  27.0 1.4 collective-permute-start.8
  28.5 1.6 collective-permute-start.3
  30.1 3.4 %collective-permute-start.2 = (bf16[1,1,1,784,128]{4,3,2,1,0:T(8,128)(2,1)S(1)}, bf16[1,1,1,784,128]{4,3,2,1,0:T(8,128)(2,1)S(1)}, u32[]{:S(2)}, u32[]{:S(2)}) collective-permute-start(bf16[1,1,1,784,128]{4,3,2,1,0:T(8,128)(2,1)S(1)} %get-tuple-element.39), channel_id=1, source_target_pairs={{0,16},{8,24},{16,0},{24,8},{1,17},{9,25},{17,1},{25,9},{2,18},{10... | collective-permute-start | bytes 602120 | tf_op jit(solution)/shard_map/ppermute | solution.py:551
  33.5 3.4 %collective-permute-done.8 = bf16[4,1,1,400,128]{4,3,0,2,1:T(8,128)(2,1)S(1)} collective-permute-done((bf16[4,1,1,400,128]{4,3,0,2,1:T(8,128)(2,1)S(1)}, bf16[4,1,1,400,128]{4,3,0,2,1:T(8,128)(2,1)S(1)}, u32[]{:S(2)}, u32[]{:S(2)}) %collective-permute-start.8) | collective-permute-done | bytes 409632 | tf_op jit(solution)/shard_map/ppermute | solution.py:551
  37.0 1.3 collective-permute-start.9
  38.4 1.6 collective-permute-start.5
  40.0 1.9 collective-permute-done.2
  41.9 0.8 collective-permute-start.4
  42.8 9.5 %collective-permute-done.4 = bf16[2,1,1,784,128]{4,3,0,2,1:T(8,128)(2,1)S(1)} collective-permute-done((bf16[2,1,1,784,128]{4,3,0,2,1:T(8,128)(2,1)S(1)}, bf16[2,1,1,784,128]{4,3,0,2,1:T(8,128)(2,1)S(1)}, u32[]{:S(2)}, u32[]{:S(2)}) %collective-permute-start.4) | collective-permute-done | bytes 401440 | tf_op jit(solution)/shard_map/ppermute | solution.py:551
  52.4 2.9 %collective-permute-done.9.refs_4_ = bf16[4,2,1,400,128]{4,3,2,1,0:T(8,128)(2,1)} collective-permute-done((bf16[4,2,1,400,128]{4,3,2,1,0:T(8,128)(2,1)S(1)}, bf16[4,2,1,400,128]{4,3,2,1,0:T(8,128)(2,1)}, u32[]{:S(2)}, u32[]{:S(2)}) %collective-permute-start.9) | collective-permute-done | bytes 819232 | tf_op jit(solution)/shard_map/ppermute | solution.py:551
  55.4 0.8 collective-permute-start.10
  56.2 1.5 collective-permute-start.6
  57.8 0.5 collective-permute-start.18
  58.4 5.6 %collective-permute-done.10 = bf16[4,1,1,400,128]{4,3,0,2,1:T(8,128)(2,1)S(1)} collective-permute-done((bf16[4,1,1,400,128]{4,3,0,2,1:T(8,128)(2,1)S(1)}, bf16[4,1,1,400,128]{4,3,0,2,1:T(8,128)(2,1)S(1)}, u32[]{:S(2)}, u32[]{:S(2)}) %collective-permute-start.10) | collective-permute-done | bytes 409632 | tf_op jit(solution)/shard_map/ppermute | solution.py:551
  64.0 2.1 collective-permute-start.11
  67.4 14.4 %collective-permute-done.7 = bf16[4,1,2,384,128]{4,3,0,2,1:T(8,128)(2,1)} collective-permute-done((bf16[4,1,2,384,128]{4,3,0,2,1:T(8,128)(2,1)S(1)}, bf16[4,1,2,384,128]{4,3,0,2,1:T(8,128)(2,1)}, u32[]{:S(2)}, u32[]{:S(2)}) %collective-permute-start.7) | collective-permute-done | bytes 786464 | tf_op jit(solution)/shard_map/ppermute | solution.py:551
  81.9 0.5 collective-permute-start.15
  82.4 3.4 %fusion.15.refs_15_.refs_18_.refs_8_ = bf16[176,6272]{1,0:T(8,128)(2,1)} fusion(s32[6272]{0:T(1024)S(1)} %get-tuple-element.113, s32[6272]{0:T(1024)S(1)} %get-tuple-element.114, s32[6272]{0:T(1024)S(1)} %get-tuple-element.115, s32[6272]{0:T(1024)S(1)} %get-tuple-element.116, s32[6272]{0:T(1024)S(1)} %get-tuple-element.117, s32[6272]{0:T(1024)S(1)} %get-tuple-element.118, ...), kind=kLoop, calls=%fused_computation.20 | loop fusion | flops 27596800 | bytes 2377088 | tf_op jit(solution)/shard_map/convert_element_type | solution.py:110
  86.4 1.0 copy.126
  87.5 1.0 copy.125
  88.5 0.9 pad.12.refs_9_
  89.4 0.9 pad.13.refs_11_
  90.2 0.9 copy.69.refs_1_
  91.2 0.9 copy.70.refs_2_
  92.1 0.9 copy.71.refs_5_
  93.0 0.9 copy.73.refs_2_
  94.0 0.9 copy.72.refs_6_
  94.9 18.2 %first.1 = (f32[256,512]{1,0:T(8,128)}, f32[8,512]{1,0:T(8,128)}, f32[256,512]{1,0:T(8,128)}, f32[256,128]{1,0:T(8,128)}, bf16[256,512]{1,0:T(8,128)(2,1)}, /*in...) custom-call(s32[1]{0:T(128)} %bitcast.refs_0_.refs_1_, ...), custom_call_target="tpu_custom_call" | custom-call | tf_op jit(solution)/shard_map/first/pallas_call | solution.py:684
  113.1 2.1 copy.74.refs_3_
  115.2 2.1 copy.75.refs_6_
  117.2 2.1 copy.76.refs_7_
  119.3 31.4 %second.1 = (f32[196,512]{1,0:T(8,128)}, f32[256,512]{1,0:T(8,128)}, bf16[16,784,128]{2,1,0:T(8,128)(2,1)}, bf16[16,784,128]{2,1,0:T(8,128)(2,1)}) custom-call(s32[1]{0:T(128)S(6)} %copy.129.refs_0_, s32[1]{0:T(128)} %bitcast.refs_0_.refs_1_, bf16[4,1,2,384,128]{4,3,2,1,0:T(8,128)(2,1)} %copy.73.refs_2_, bf16[4,1,2,384,128]{4,3,2,1,0:T(8,128)(2,1)} %copy.74.refs_3_, ...), custom_call_target="tpu_custom_call" | custom-call | tf_op jit(solution)/shard_map/second/pallas_call | solution.py:699
  150.7 20.7 %third.1 = (f32[196,512]{1,0:T(8,128)}, bf16[16,784,128]{2,1,0:T(8,128)(2,1)}, bf16[16,784,128]{2,1,0:T(8,128)(2,1)}) custom-call(s32[1]{0:T(128)S(6)} %copy.129.refs_0_, s32[1]{0:T(128)} %bitcast.refs_0_.refs_1_, f32[256,512]{1,0:T(8,128)} %get-tuple-element.48.refs_2_, f32[8,512]{1,0:T(8,128)} %get-tuple-element.49.refs_3_, ...), custom_call_target="tpu_custom_call" | custom-call | tf_op jit(solution)/shard_map/third/pallas_call | solution.py:741
  171.9 5.5 %collective-permute-done.21 = bf16[16,784,128]{2,1,0:T(8,128)(2,1)S(1)} collective-permute-done((bf16[16,784,128]{2,1,0:T(8,128)(2,1)}, bf16[16,784,128]{2,1,0:T(8,128)(2,1)S(1)}, u32[]{:S(2)}, u32[]{:S(2)}) %collective-permute-start.21) | collective-permute-done | bytes 3211296 | tf_op jit(solution)/shard_map/ppermute | solution.py:551
  177.3 2.0 fusion.18
  179.4 0.9 collective-permute-start.22
  180.9 1.8 collective-permute-start.23
  183.2 0.5 collective-permute-start.28
  184.2 1.5 collective-permute-start.29
  185.7 14.2 %collective-permute-done.22 = bf16[4,2,1,384,128]{4,3,0,1,2:T(8,128)(2,1)S(1)} collective-permute-done((bf16[4,2,1,384,128]{4,3,0,1,2:T(8,128)(2,1)S(1)}, bf16[4,2,1,384,128]{4,3,0,1,2:T(8,128)(2,1)S(1)}, u32[]{:S(2)}, u32[]{:S(2)}) %collective-permute-start.22) | collective-permute-done | bytes 786464 | tf_op jit(solution)/shard_map/ppermute | solution.py:551
  200.1 1.1 collective-permute-start.24
  201.1 14.8 %collective-permute-done.28 = bf16[4,2,1,384,128]{4,3,0,1,2:T(8,128)(2,1)S(1)} collective-permute-done((bf16[4,2,1,384,128]{4,3,0,1,2:T(8,128)(2,1)S(1)}, bf16[4,2,1,384,128]{4,3,0,1,2:T(8,128)(2,1)S(1)}, u32[]{:S(2)}, u32[]{:S(2)}) %collective-permute-start.28) | collective-permute-done | bytes 786464 | tf_op jit(solution)/shard_map/ppermute | solution.py:551
  216.2 1.2 collective-permute-start.25
  217.4 2.2 collective-permute-done.29
  219.8 1.2 collective-permute-start.31
  221.1 1.1 collective-permute-start.30
  222.2 5.9 %collective-permute-done.24 = bf16[4,1,1,384,128]{4,3,0,2,1:T(8,128)(2,1)S(1)} collective-permute-done((bf16[4,1,1,384,128]{4,3,0,2,1:T(8,128)(2,1)S(1)}, bf16[4,1,1,384,128]{4,3,0,2,1:T(8,128)(2,1)S(1)}, u32[]{:S(2)}, u32[]{:S(2)}) %collective-permute-start.24) | collective-permute-done | bytes 393248 | tf_op jit(solution)/shard_map/ppermute | solution.py:551
  228.0 0.5 collective-permute-done.25
  228.8 3.4 %collective-permute-start.26 = (bf16[2,1,1,784,128]{4,3,0,2,1:T(8,128)(2,1)S(1)}, bf16[2,1,1,784,128]{4,3,0,2,1:T(8,128)(2,1)S(1)}, u32[]{:S(2)}, u32[]{:S(2)}) collective-permute-start(bf16[2,1,1,784,128]{4,3,0,2,1:T(8,128)(2,1)S(1)} %slice_bitcast_fusion.12), channel_id=1, source_target_pairs={{0,8},{8,0},{16,24},{24,16},{1,9},{9,1},{17,25},{25,17},{2,10},{10... | collective-permute-start | bytes 1204232 | tf_op jit(solution)/shard_map/ppermute | solution.py:551
  232.2 1.2 copy.89
  233.4 1.2 copy.90
  234.6 1.0 collective-permute-done.30
  235.9 3.7 %collective-permute-start.32 = (bf16[2,1,1,784,128]{4,3,0,2,1:T(8,128)(2,1)S(1)}, bf16[2,1,1,784,128]{4,3,0,2,1:T(8,128)(2,1)S(1)}, u32[]{:S(2)}, u32[]{:S(2)}) collective-permute-start(bf16[2,1,1,784,128]{4,3,0,2,1:T(8,128)(2,1)S(1)} %slice_bitcast_fusion.10), channel_id=1, source_target_pairs={{0,8},{8,0},{16,24},{24,16},{1,9},{9,1},{17,25},{25,17},{2,10},{10... | collective-permute-start | bytes 1204232 | tf_op jit(solution)/shard_map/ppermute | solution.py:551
  240.1 4.3 %collective-permute-start.27 = (bf16[1,1,1,784,128]{4,3,2,1,0:T(8,128)(2,1)S(1)}, bf16[1,1,1,784,128]{4,3,2,1,0:T(8,128)(2,1)S(1)}, u32[]{:S(2)}, u32[]{:S(2)}) collective-permute-start(bf16[1,1,1,784,128]{4,3,2,1,0:T(8,128)(2,1)S(1)} %slice_bitcast_fusion.18), channel_id=1, source_target_pairs={{0,16},{8,24},{16,0},{24,8},{1,17},{9,25},{17,1},{25,9},{2,18},{10... | collective-permute-start | bytes 602120 | tf_op jit(solution)/shard_map/ppermute | solution.py:551
  244.4 8.4 %collective-permute-done.32 = bf16[2,1,1,784,128]{4,3,0,2,1:T(8,128)(2,1)S(1)} collective-permute-done((bf16[2,1,1,784,128]{4,3,0,2,1:T(8,128)(2,1)S(1)}, bf16[2,1,1,784,128]{4,3,0,2,1:T(8,128)(2,1)S(1)}, u32[]{:S(2)}, u32[]{:S(2)}) %collective-permute-start.32) | collective-permute-done | bytes 401440 | tf_op jit(solution)/shard_map/ppermute | solution.py:551
  252.9 2.7 %collective-permute-start.33 = (bf16[1,1,1,784,128]{4,3,2,1,0:T(8,128)(2,1)S(1)}, bf16[1,1,1,784,128]{4,3,2,1,0:T(8,128)(2,1)S(1)}, u32[]{:S(2)}, u32[]{:S(2)}) collective-permute-start(bf16[1,1,1,784,128]{4,3,2,1,0:T(8,128)(2,1)S(1)} %slice_bitcast_fusion.16), channel_id=1, source_target_pairs={{0,16},{8,24},{16,0},{24,8},{1,17},{9,25},{17,1},{25,9},{2,18},{10... | collective-permute-start | bytes 602120 | tf_op jit(solution)/shard_map/ppermute | solution.py:551
  256.1 8.9 %collective-permute-done.33 = bf16[1,1,1,784,128]{4,3,2,1,0:T(8,128)(2,1)S(1)} collective-permute-done((bf16[1,1,1,784,128]{4,3,2,1,0:T(8,128)(2,1)S(1)}, bf16[1,1,1,784,128]{4,3,2,1,0:T(8,128)(2,1)S(1)}, u32[]{:S(2)}, u32[]{:S(2)}) %collective-permute-start.33) | collective-permute-done | bytes 200736 | tf_op jit(solution)/shard_map/ppermute | solution.py:551
  265.5 4.3 %multiply_subtract_fusion = (f32[2,98688]{1,0:T(2,128)}, f32[2,98688]{1,0:T(2,128)}, f32[2,98688]{1,0:T(2,128)}, f32[2,98688]{1,0:T(2,128)}) fusion(f32[2,98688]{1,0:T(2,128)S(1)} %copy-done.4, f32[2,98688]{1,0:T(2,128)S(1)} %copy-done.6, f32[2,98688]{1,0:T(2,128)S(1)} %copy-done.7, f32[1,98688]{1,0:T(1,128)S(1)} %bitcast.208, f32[1,98688]{1,0:T(1,128)S(1)} %bitcast.207), kind=kLoop, calls=%fused_computation.45 | loop fusion | flops 3158016 | bytes 6316032 | tf_op jit(solution)/shard_map/sub | solution.py:622
  (114 shorter events, 7.2 us)
Async XLA Ops:
  2.8 13.4 %collective-permute-start = (bf16[1,1,1,784,128]{4,3,2,1,0:T(8,128)(2,1)S(1)}, bf16[1,1,1,784,128]{4,3,2,1,0:T(8,128)(2,1)S(1)}, u32[]{:S(2)}, u32[]{:S(2)}) collective-permute-start(bf16[1,1,1,784,128]{4,3,2,1,0:T(8,128)(2,1)S(1)} %get-tuple-element.111), channel_id=1, source_target_pairs={{0,16},{8,24},{16,0},{24,8},{1,17},{9,25},{17,1},{25,9},{2,18},{10... | collective-permute-start | bytes 602120 | tf_op jit(solution)/shard_map/ppermute | solution.py:551
  16.3 10.5 %collective-permute-start.1 = (bf16[2,1,1,784,128]{4,3,0,2,1:T(8,128)(2,1)S(1)}, bf16[2,1,1,784,128]{4,3,0,2,1:T(8,128)(2,1)S(1)}, u32[]{:S(2)}, u32[]{:S(2)}) collective-permute-start(bf16[2,1,1,784,128]{4,3,0,2,1:T(8,128)(2,1)S(1)} %get-tuple-element.109), channel_id=1, source_target_pairs={{0,8},{8,0},{16,24},{24,16},{1,9},{9,1},{17,25},{25,17},{2,10},{10... | collective-permute-start | bytes 1204232 | tf_op jit(solution)/shard_map/ppermute | solution.py:551
  27.0 9.8 %collective-permute-start.8 = (bf16[4,1,1,400,128]{4,3,0,2,1:T(8,128)(2,1)S(1)}, bf16[4,1,1,400,128]{4,3,0,2,1:T(8,128)(2,1)S(1)}, u32[]{:S(2)}, u32[]{:S(2)}) collective-permute-start(bf16[4,1,1,400,128]{4,3,0,2,1:T(8,128)(2,1)S(1)} %get-tuple-element.101), channel_id=1, source_target_pairs={{0,4},{4,0},{1,5},{5,1},{2,6},{6,2},{3,7},{7,3},{8,12},{12,8},{9,1... | collective-permute-start | bytes 1228808 | tf_op jit(solution)/shard_map/ppermute | solution.py:551
  28.5 9.8 %collective-permute-start.3 = (bf16[4,1,1,384,128]{4,3,0,2,1:T(8,128)(2,1)S(1)}, bf16[4,1,1,384,128]{4,3,0,2,1:T(8,128)(2,1)S(1)}, u32[]{:S(2)}, u32[]{:S(2)}) collective-permute-start(bf16[4,1,1,384,128]{4,3,0,2,1:T(8,128)(2,1)S(1)} %get-tuple-element.103), channel_id=1, source_target_pairs={{0,2},{2,0},{1,3},{3,1},{4,6},{6,4},{5,7},{7,5},{8,10},{10,8},{9,1... | collective-permute-start | bytes 1179656 | tf_op jit(solution)/shard_map/ppermute | solution.py:551
  30.1 11.7 %collective-permute-start.2 = (bf16[1,1,1,784,128]{4,3,2,1,0:T(8,128)(2,1)S(1)}, bf16[1,1,1,784,128]{4,3,2,1,0:T(8,128)(2,1)S(1)}, u32[]{:S(2)}, u32[]{:S(2)}) collective-permute-start(bf16[1,1,1,784,128]{4,3,2,1,0:T(8,128)(2,1)S(1)} %get-tuple-element.39), channel_id=1, source_target_pairs={{0,16},{8,24},{16,0},{24,8},{1,17},{9,25},{17,1},{25,9},{2,18},{10... | collective-permute-start | bytes 602120 | tf_op jit(solution)/shard_map/ppermute | solution.py:551
  37.0 20.8 %copy-start.1 = (bf16[4,2,1,400,128]{4,3,2,1,0:T(8,128)(2,1)}, bf16[4,2,1,400,128]{4,3,2,1,0:T(8,128)(2,1)S(1)}, u32[]{:S(2)}) copy-start(bf16[4,2,1,400,128]{4,3,2,1,0:T(8,128)(2,1)S(1)} %maximum_bitcast_fusion.refs_3_) | copy-start | bytes 2457604
  37.0 18.4 %collective-permute-start.9 = (bf16[4,2,1,400,128]{4,3,2,1,0:T(8,128)(2,1)S(1)}, bf16[4,2,1,400,128]{4,3,2,1,0:T(8,128)(2,1)}, u32[]{:S(2)}, u32[]{:S(2)}) collective-permute-start(bf16[4,2,1,400,128]{4,3,2,1,0:T(8,128)(2,1)S(1)} %maximum_bitcast_fusion.refs_3_), channel_id=1, source_target_pairs={{0,2},{2,0},{1,3},{3,1},{4,6},{6,4},{5,7},{7,5},{8,10},{10,8},{9,1... | collective-permute-start | bytes 2457608 | tf_op jit(solution)/shard_map/ppermute | solution.py:551
  38.4 17.8 %collective-permute-start.5 = (bf16[4,1,2,384,128]{4,3,0,2,1:T(8,128)(2,1)S(1)}, bf16[4,1,2,384,128]{4,3,0,2,1:T(8,128)(2,1)S(1)}, u32[]{:S(2)}, u32[]{:S(2)}) collective-permute-start(bf16[4,1,2,384,128]{4,3,0,2,1:T(8,128)(2,1)S(1)} %maximum_bitcast_fusion.2), channel_id=1, source_target_pairs={{0,4},{4,0},{1,5},{5,1},{2,6},{6,2},{3,7},{7,3},{8,12},{12,8},{9,1... | collective-permute-start | bytes 2359304 | tf_op jit(solution)/shard_map/ppermute | solution.py:551
  41.9 10.4 %collective-permute-start.4 = (bf16[2,1,1,784,128]{4,3,0,2,1:T(8,128)(2,1)S(1)}, bf16[2,1,1,784,128]{4,3,0,2,1:T(8,128)(2,1)S(1)}, u32[]{:S(2)}, u32[]{:S(2)}) collective-permute-start(bf16[2,1,1,784,128]{4,3,0,2,1:T(8,128)(2,1)S(1)} %maximum_bitcast_fusion.4), channel_id=1, source_target_pairs={{0,8},{8,0},{16,24},{24,16},{1,9},{9,1},{17,25},{25,17},{2,10},{10... | collective-permute-start | bytes 1204232 | tf_op jit(solution)/shard_map/ppermute | solution.py:551
  55.4 8.6 %collective-permute-start.10 = (bf16[4,1,1,400,128]{4,3,0,2,1:T(8,128)(2,1)S(1)}, bf16[4,1,1,400,128]{4,3,0,2,1:T(8,128)(2,1)S(1)}, u32[]{:S(2)}, u32[]{:S(2)}) collective-permute-start(bf16[4,1,1,400,128]{4,3,0,2,1:T(8,128)(2,1)S(1)} %slice.164), channel_id=1, source_target_pairs={{0,4},{4,0},{1,5},{5,1},{2,6},{6,2},{3,7},{7,3},{8,12},{12,8},{9,1... | collective-permute-start | bytes 1228808 | tf_op jit(solution)/shard_map/ppermute | solution.py:551
  56.2 10.0 %collective-permute-start.6 = (bf16[4,1,1,384,128]{4,3,0,2,1:T(8,128)(2,1)S(1)}, bf16[4,1,1,384,128]{4,3,0,2,1:T(8,128)(2,1)S(1)}, u32[]{:S(2)}, u32[]{:S(2)}) collective-permute-start(bf16[4,1,1,384,128]{4,3,0,2,1:T(8,128)(2,1)S(1)} %slice.163), channel_id=1, source_target_pairs={{0,2},{2,0},{1,3},{3,1},{4,6},{6,4},{5,7},{7,5},{8,10},{10,8},{9,1... | collective-permute-start | bytes 1179656 | tf_op jit(solution)/shard_map/ppermute | solution.py:551
  57.8 8.9 %collective-permute-start.16 = (bf16[4,1,2,384,128]{4,3,0,2,1:T(8,128)(2,1)S(1)}, bf16[4,1,2,384,128]{4,3,0,2,1:T(8,128)(2,1)S(1)}, u32[]{:S(2)}, u32[]{:S(2)}) collective-permute-start(bf16[4,1,2,384,128]{4,3,0,2,1:T(8,128)(2,1)S(1)} %maximum_bitcast_fusion.2), channel_id=1, source_target_pairs={{0,1},{1,0},{2,3},{3,2},{4,5},{5,4},{6,7},{7,6},{8,9},{9,8},{10,11... | collective-permute-start | bytes 2359304 | tf_op jit(solution)/shard_map/ppermute | solution.py:551
  57.8 9.0 %collective-permute-start.18 = (bf16[4,2,1,400,128]{4,3,2,1,0:T(8,128)(2,1)S(1)}, bf16[4,2,1,400,128]{4,3,2,1,0:T(8,128)(2,1)S(1)}, u32[]{:S(2)}, u32[]{:S(2)}) collective-permute-start(bf16[4,2,1,400,128]{4,3,2,1,0:T(8,128)(2,1)S(1)} %maximum_bitcast_fusion.refs_3_), channel_id=1, source_target_pairs={{0,1},{1,0},{2,3},{3,2},{4,5},{5,4},{6,7},{7,6},{8,9},{9,8},{10,11... | collective-permute-start | bytes 2457608 | tf_op jit(solution)/shard_map/ppermute | solution.py:551
  58.3 9.0 %collective-permute-start.17 = (bf16[4,1,2,384,128]{4,3,0,2,1:T(8,128)(2,1)S(1)}, bf16[4,1,2,384,128]{4,3,0,2,1:T(8,128)(2,1)S(1)}, u32[]{:S(2)}, u32[]{:S(2)}) collective-permute-start(bf16[4,1,2,384,128]{4,3,0,2,1:T(8,128)(2,1)S(1)} %collective-permute-done.5), channel_id=1, source_target_pairs={{0,1},{1,0},{2,3},{3,2},{4,5},{5,4},{6,7},{7,6},{8,9},{9,8},{10,11... | collective-permute-start | bytes 2359304 | tf_op jit(solution)/shard_map/ppermute | solution.py:551
  64.0 22.4 %copy-start = (bf16[4,2,1,400,128]{4,3,2,1,0:T(8,128)(2,1)}, bf16[4,2,1,400,128]{4,3,2,1,0:T(8,128)(2,1)S(1)}, u32[]{:S(2)}) copy-start(bf16[4,2,1,400,128]{4,3,2,1,0:T(8,128)(2,1)S(1)} %maximum_bitcast_fusion.1.refs_4_) | copy-start | bytes 2457604
  64.0 17.8 %collective-permute-start.11 = (bf16[4,2,1,400,128]{4,3,2,1,0:T(8,128)(2,1)S(1)}, bf16[4,2,1,400,128]{4,3,2,1,0:T(8,128)(2,1)}, u32[]{:S(2)}, u32[]{:S(2)}) collective-permute-start(bf16[4,2,1,400,128]{4,3,2,1,0:T(8,128)(2,1)S(1)} %maximum_bitcast_fusion.1.refs_4_), channel_id=1, source_target_pairs={{0,2},{2,0},{1,3},{3,1},{4,6},{6,4},{5,7},{7,5},{8,10},{10,8},{9,1... | collective-permute-start | bytes 2457608 | tf_op jit(solution)/shard_map/ppermute | solution.py:551
  66.2 15.6 %collective-permute-start.7 = (bf16[4,1,2,384,128]{4,3,0,2,1:T(8,128)(2,1)S(1)}, bf16[4,1,2,384,128]{4,3,0,2,1:T(8,128)(2,1)}, u32[]{:S(2)}, u32[]{:S(2)}) collective-permute-start(bf16[4,1,2,384,128]{4,3,0,2,1:T(8,128)(2,1)S(1)} %maximum_bitcast_fusion.3), channel_id=1, source_target_pairs={{0,4},{4,0},{1,5},{5,1},{2,6},{6,2},{3,7},{7,3},{8,12},{12,8},{9,1... | collective-permute-start | bytes 2359304 | tf_op jit(solution)/shard_map/ppermute | solution.py:551
  66.7 15.7 %copy-start.8 = (bf16[4,1,2,384,128]{4,3,0,2,1:T(8,128)(2,1)}, bf16[4,1,2,384,128]{4,3,0,2,1:T(8,128)(2,1)S(1)}, u32[]{:S(2)}) copy-start(bf16[4,1,2,384,128]{4,3,0,2,1:T(8,128)(2,1)S(1)} %collective-permute-done.16) | copy-start | bytes 2359300
  66.7 28.2 %collective-permute-start.19 = (bf16[4,2,1,400,128]{4,3,2,1,0:T(8,128)(2,1)}, bf16[4,2,1,400,128]{4,3,2,1,0:T(8,128)(2,1)}, u32[]{:S(2)}, u32[]{:S(2)}) collective-permute-start(bf16[4,2,1,400,128]{4,3,2,1,0:T(8,128)(2,1)} %collective-permute-done.9.refs_4_), channel_id=1, source_target_pairs={{0,1},{1,0},{2,3},{3,2},{4,5},{5,4},{6,7},{7,6},{8,9},{9,8},{10,11... | collective-permute-start | bytes 2457608 | tf_op jit(solution)/shard_map/ppermute | solution.py:551
  66.8 15.0 %copy-start.5 = (bf16[4,2,1,400,128]{4,3,2,1,0:T(8,128)(2,1)}, bf16[4,2,1,400,128]{4,3,2,1,0:T(8,128)(2,1)S(1)}, u32[]{:S(2)}) copy-start(bf16[4,2,1,400,128]{4,3,2,1,0:T(8,128)(2,1)S(1)} %collective-permute-done.18.refs_7_) | copy-start | bytes 2457604
  66.8 48.3 %collective-permute-start.12 = (bf16[4,1,2,384,128]{4,3,0,2,1:T(8,128)(2,1)S(1)}, bf16[4,1,2,384,128]{4,3,0,2,1:T(8,128)(2,1)}, u32[]{:S(2)}, u32[]{:S(2)}) collective-permute-start(bf16[4,1,2,384,128]{4,3,0,2,1:T(8,128)(2,1)S(1)} %maximum_bitcast_fusion.3), channel_id=1, source_target_pairs={{0,1},{1,0},{2,3},{3,2},{4,5},{5,4},{6,7},{7,6},{8,9},{9,8},{10,11... | collective-permute-start | bytes 2359304 | tf_op jit(solution)/shard_map/ppermute | solution.py:551
  67.3 15.1 %copy-start.10 = (bf16[4,1,2,384,128]{4,3,0,2,1:T(8,128)(2,1)}, bf16[4,1,2,384,128]{4,3,0,2,1:T(8,128)(2,1)S(1)}, u32[]{:S(2)}) copy-start(bf16[4,1,2,384,128]{4,3,0,2,1:T(8,128)(2,1)S(1)} %collective-permute-done.17) | copy-start | bytes 2359300
  67.3 52.0 %collective-permute-start.14 = (bf16[4,2,1,400,128]{4,3,2,1,0:T(8,128)(2,1)S(1)}, bf16[4,2,1,400,128]{4,3,2,1,0:T(8,128)(2,1)}, u32[]{:S(2)}, u32[]{:S(2)}) collective-permute-start(bf16[4,2,1,400,128]{4,3,2,1,0:T(8,128)(2,1)S(1)} %maximum_bitcast_fusion.1.refs_4_), channel_id=1, source_target_pairs={{0,1},{1,0},{2,3},{3,2},{4,5},{5,4},{6,7},{7,6},{8,9},{9,8},{10,11... | collective-permute-start | bytes 2457608 | tf_op jit(solution)/shard_map/ppermute | solution.py:551
  81.9 35.4 %collective-permute-start.13 = (bf16[4,1,2,384,128]{4,3,0,2,1:T(8,128)(2,1)}, bf16[4,1,2,384,128]{4,3,0,2,1:T(8,128)(2,1)}, u32[]{:S(2)}, u32[]{:S(2)}) collective-permute-start(bf16[4,1,2,384,128]{4,3,0,2,1:T(8,128)(2,1)} %collective-permute-done.7), channel_id=1, source_target_pairs={{0,1},{1,0},{2,3},{3,2},{4,5},{5,4},{6,7},{7,6},{8,9},{9,8},{10,11... | collective-permute-start | bytes 2359304 | tf_op jit(solution)/shard_map/ppermute | solution.py:551
  81.9 37.4 %collective-permute-start.15 = (bf16[4,2,1,400,128]{4,3,2,1,0:T(8,128)(2,1)}, bf16[4,2,1,400,128]{4,3,2,1,0:T(8,128)(2,1)}, u32[]{:S(2)}, u32[]{:S(2)}) collective-permute-start(bf16[4,2,1,400,128]{4,3,2,1,0:T(8,128)(2,1)} %collective-permute-done.11.refs_5_), channel_id=1, source_target_pairs={{0,1},{1,0},{2,3},{3,2},{4,5},{5,4},{6,7},{7,6},{8,9},{9,8},{10,11... | collective-permute-start | bytes 2457608 | tf_op jit(solution)/shard_map/ppermute | solution.py:551
  90.2 1.9 copy-start.9
  91.2 2.8 %copy-start.11 = (bf16[4,1,2,384,128]{4,3,0,2,1:T(8,128)(2,1)S(1)}, bf16[4,1,2,384,128]{4,3,0,2,1:T(8,128)(2,1)}, u32[]{:S(2)}) copy-start(bf16[4,1,2,384,128]{4,3,0,2,1:T(8,128)(2,1)} %copy-done.10) | copy-start | bytes 2359300
  150.7 20.7 %copy-start.14 = (bf16[16,784,128]{2,1,0:T(8,128)(2,1)S(1)}, bf16[16,784,128]{2,1,0:T(8,128)(2,1)}, u32[]{:S(2)}) copy-start(bf16[16,784,128]{2,1,0:T(8,128)(2,1)} %get-tuple-element.47) | copy-start | bytes 9633796
  171.3 6.0 %collective-permute-start.21 = (bf16[16,784,128]{2,1,0:T(8,128)(2,1)}, bf16[16,784,128]{2,1,0:T(8,128)(2,1)S(1)}, u32[]{:S(2)}, u32[]{:S(2)}) collective-permute-start(bf16[16,784,128]{2,1,0:T(8,128)(2,1)} %get-tuple-element.69), channel_id=1, source_target_pairs={{0,1},{1,0},{2,3},{3,2},{4,5},{5,4},{6,7},{7,6},{8,9},{9,8},{10,11... | collective-permute-start | bytes 9633800 | tf_op jit(solution)/shard_map/ppermute | solution.py:551
  171.4 11.3 %collective-permute-start.20 = (bf16[16,784,128]{2,1,0:T(8,128)(2,1)S(1)}, bf16[16,784,128]{2,1,0:T(8,128)(2,1)S(1)}, u32[]{:S(2)}, u32[]{:S(2)}) collective-permute-start(bf16[16,784,128]{2,1,0:T(8,128)(2,1)S(1)} %copy-done.14), channel_id=1, source_target_pairs={{0,1},{1,0},{2,3},{3,2},{4,5},{5,4},{6,7},{7,6},{8,9},{9,8},{10,11... | collective-permute-start | bytes 9633800 | tf_op jit(solution)/shard_map/ppermute | solution.py:551
  177.3 3.1 %copy-start.3 = (bf16[16,784,128]{2,1,0:T(8,128)(2,1)S(1)}, bf16[16,784,128]{2,1,0:T(8,128)(2,1)}, u32[]{:S(2)}) copy-start(bf16[16,784,128]{2,1,0:T(8,128)(2,1)} %get-tuple-element.68) | copy-start | bytes 9633796
  179.4 3.3 %copy-start.2 = (bf16[16,784,128]{2,1,0:T(8,128)(2,1)S(1)}, bf16[16,784,128]{2,1,0:T(8,128)(2,1)}, u32[]{:S(2)}) copy-start(bf16[16,784,128]{2,1,0:T(8,128)(2,1)} %get-tuple-element.46) | copy-start | bytes 9633796
  179.4 20.5 %collective-permute-start.22 = (bf16[4,2,1,384,128]{4,3,0,1,2:T(8,128)(2,1)S(1)}, bf16[4,2,1,384,128]{4,3,0,1,2:T(8,128)(2,1)S(1)}, u32[]{:S(2)}, u32[]{:S(2)}) collective-permute-start(bf16[4,2,1,384,128]{4,3,0,1,2:T(8,128)(2,1)S(1)} %slice_bitcast_fusion.5), channel_id=1, source_target_pairs={{0,2},{2,0},{1,3},{3,1},{4,6},{6,4},{5,7},{7,5},{8,10},{10,8},{9,1... | collective-permute-start | bytes 2359304 | tf_op jit(solution)/shard_map/ppermute | solution.py:551
  180.9 35.1 %collective-permute-start.23 = (bf16[4,1,2,400,128]{4,3,0,2,1:T(8,128)(2,1)S(1)}, bf16[4,1,2,400,128]{4,3,0,2,1:T(8,128)(2,1)S(1)}, u32[]{:S(2)}, u32[]{:S(2)}) collective-permute-start(bf16[4,1,2,400,128]{4,3,0,2,1:T(8,128)(2,1)S(1)} %slice_bitcast_fusion.1), channel_id=1, source_target_pairs={{0,4},{4,0},{1,5},{5,1},{2,6},{6,2},{3,7},{7,3},{8,12},{12,8},{9,1... | collective-permute-start | bytes 2457608 | tf_op jit(solution)/shard_map/ppermute | solution.py:551
  183.2 32.7 %collective-permute-start.28 = (bf16[4,2,1,384,128]{4,3,0,1,2:T(8,128)(2,1)S(1)}, bf16[4,2,1,384,128]{4,3,0,1,2:T(8,128)(2,1)S(1)}, u32[]{:S(2)}, u32[]{:S(2)}) collective-permute-start(bf16[4,2,1,384,128]{4,3,0,1,2:T(8,128)(2,1)S(1)} %slice_bitcast_fusion.4), channel_id=1, source_target_pairs={{0,2},{2,0},{1,3},{3,1},{4,6},{6,4},{5,7},{7,5},{8,10},{10,8},{9,1... | collective-permute-start | bytes 2359304 | tf_op jit(solution)/shard_map/ppermute | solution.py:551
  184.2 35.4 %collective-permute-start.29 = (bf16[4,1,2,400,128]{4,3,0,2,1:T(8,128)(2,1)S(1)}, bf16[4,1,2,400,128]{4,3,0,2,1:T(8,128)(2,1)S(1)}, u32[]{:S(2)}, u32[]{:S(2)}) collective-permute-start(bf16[4,1,2,400,128]{4,3,0,2,1:T(8,128)(2,1)S(1)} %slice_bitcast_fusion), channel_id=1, source_target_pairs={{0,4},{4,0},{1,5},{5,1},{2,6},{6,2},{3,7},{7,3},{8,12},{12,8},{9,1... | collective-permute-start | bytes 2457608 | tf_op jit(solution)/shard_map/ppermute | solution.py:551
  200.1 28.0 %collective-permute-start.24 = (bf16[4,1,1,384,128]{4,3,0,2,1:T(8,128)(2,1)S(1)}, bf16[4,1,1,384,128]{4,3,0,2,1:T(8,128)(2,1)S(1)}, u32[]{:S(2)}, u32[]{:S(2)}) collective-permute-start(bf16[4,1,1,384,128]{4,3,0,2,1:T(8,128)(2,1)S(1)} %get-tuple-element.104), channel_id=1, source_target_pairs={{0,4},{4,0},{1,5},{5,1},{2,6},{6,2},{3,7},{7,3},{8,12},{12,8},{9,1... | collective-permute-start | bytes 1179656 | tf_op jit(solution)/shard_map/ppermute | solution.py:551
  216.2 12.4 %collective-permute-start.25 = (bf16[4,1,1,400,128]{4,3,0,2,1:T(8,128)(2,1)S(1)}, bf16[4,1,1,400,128]{4,3,0,2,1:T(8,128)(2,1)S(1)}, u32[]{:S(2)}, u32[]{:S(2)}) collective-permute-start(bf16[4,1,1,400,128]{4,3,0,2,1:T(8,128)(2,1)S(1)} %get-tuple-element.96), channel_id=1, source_target_pairs={{0,2},{2,0},{1,3},{3,1},{4,6},{6,4},{5,7},{7,5},{8,10},{10,8},{9,1... | collective-permute-start | bytes 1228808 | tf_op jit(solution)/shard_map/ppermute | solution.py:551
  219.8 12.4 %copy-start.12 = (f32[196,512]{1,0:T(8,128)S(1)}, f32[196,512]{1,0:T(8,128)}, u32[]{:S(2)}) copy-start(f32[196,512]{1,0:T(8,128)} %get-tuple-element.44) | copy-start | bytes 1204228
  219.8 15.9 %collective-permute-start.31 = (bf16[4,1,1,400,128]{4,3,0,2,1:T(8,128)(2,1)S(1)}, bf16[4,1,1,400,128]{4,3,0,2,1:T(8,128)(2,1)S(1)}, u32[]{:S(2)}, u32[]{:S(2)}) collective-permute-start(bf16[4,1,1,400,128]{4,3,0,2,1:T(8,128)(2,1)S(1)} %get-tuple-element.98), channel_id=1, source_target_pairs={{0,2},{2,0},{1,3},{3,1},{4,6},{6,4},{5,7},{7,5},{8,10},{10,8},{9,1... | collective-permute-start | bytes 1228808 | tf_op jit(solution)/shard_map/ppermute | solution.py:551
  221.1 12.3 %copy-start.13 = (f32[196,512]{1,0:T(8,128)S(1)}, f32[196,512]{1,0:T(8,128)}, u32[]{:S(2)}) copy-start(f32[196,512]{1,0:T(8,128)} %get-tuple-element.67) | copy-start | bytes 1204228
  221.1 14.5 %collective-permute-start.30 = (bf16[4,1,1,384,128]{4,3,0,2,1:T(8,128)(2,1)S(1)}, bf16[4,1,1,384,128]{4,3,0,2,1:T(8,128)(2,1)S(1)}, u32[]{:S(2)}, u32[]{:S(2)}) collective-permute-start(bf16[4,1,1,384,128]{4,3,0,2,1:T(8,128)(2,1)S(1)} %get-tuple-element.106), channel_id=1, source_target_pairs={{0,4},{4,0},{1,5},{5,1},{2,6},{6,2},{3,7},{7,3},{8,12},{12,8},{9,1... | collective-permute-start | bytes 1179656 | tf_op jit(solution)/shard_map/ppermute | solution.py:551
  228.8 11.2 %collective-permute-start.26 = (bf16[2,1,1,784,128]{4,3,0,2,1:T(8,128)(2,1)S(1)}, bf16[2,1,1,784,128]{4,3,0,2,1:T(8,128)(2,1)S(1)}, u32[]{:S(2)}, u32[]{:S(2)}) collective-permute-start(bf16[2,1,1,784,128]{4,3,0,2,1:T(8,128)(2,1)S(1)} %slice_bitcast_fusion.12), channel_id=1, source_target_pairs={{0,8},{8,0},{16,24},{24,16},{1,9},{9,1},{17,25},{25,17},{2,10},{10... | collective-permute-start | bytes 1204232 | tf_op jit(solution)/shard_map/ppermute | solution.py:551
  235.9 16.8 %collective-permute-start.32 = (bf16[2,1,1,784,128]{4,3,0,2,1:T(8,128)(2,1)S(1)}, bf16[2,1,1,784,128]{4,3,0,2,1:T(8,128)(2,1)S(1)}, u32[]{:S(2)}, u32[]{:S(2)}) collective-permute-start(bf16[2,1,1,784,128]{4,3,0,2,1:T(8,128)(2,1)S(1)} %slice_bitcast_fusion.10), channel_id=1, source_target_pairs={{0,8},{8,0},{16,24},{24,16},{1,9},{9,1},{17,25},{25,17},{2,10},{10... | collective-permute-start | bytes 1204232 | tf_op jit(solution)/shard_map/ppermute | solution.py:551
  240.1 15.5 %collective-permute-start.27 = (bf16[1,1,1,784,128]{4,3,2,1,0:T(8,128)(2,1)S(1)}, bf16[1,1,1,784,128]{4,3,2,1,0:T(8,128)(2,1)S(1)}, u32[]{:S(2)}, u32[]{:S(2)}) collective-permute-start(bf16[1,1,1,784,128]{4,3,2,1,0:T(8,128)(2,1)S(1)} %slice_bitcast_fusion.18), channel_id=1, source_target_pairs={{0,16},{8,24},{16,0},{24,8},{1,17},{9,25},{17,1},{25,9},{2,18},{10... | collective-permute-start | bytes 602120 | tf_op jit(solution)/shard_map/ppermute | solution.py:551
  252.9 12.6 %copy-start.4 = (f32[2,98688]{1,0:T(2,128)S(1)}, f32[2,98688]{1,0:T(2,128)}, u32[]{:S(2)}) copy-start(f32[2,98688]{1,0:T(2,128)} %param.17) | copy-start | bytes 2368516
  252.9 12.6 %copy-start.6 = (f32[2,98688]{1,0:T(2,128)S(1)}, f32[2,98688]{1,0:T(2,128)}, u32[]{:S(2)}) copy-start(f32[2,98688]{1,0:T(2,128)} %param.18) | copy-start | bytes 2368516
  252.9 12.6 %copy-start.7 = (f32[2,98688]{1,0:T(2,128)S(1)}, f32[2,98688]{1,0:T(2,128)}, u32[]{:S(2)}) copy-start(f32[2,98688]{1,0:T(2,128)} %param.19) | copy-start | bytes 2368516
  252.9 12.1 %collective-permute-start.33 = (bf16[1,1,1,784,128]{4,3,2,1,0:T(8,128)(2,1)S(1)}, bf16[1,1,1,784,128]{4,3,2,1,0:T(8,128)(2,1)S(1)}, u32[]{:S(2)}, u32[]{:S(2)}) collective-permute-start(bf16[1,1,1,784,128]{4,3,2,1,0:T(8,128)(2,1)S(1)} %slice_bitcast_fusion.16), channel_id=1, source_target_pairs={{0,16},{8,24},{16,0},{24,8},{1,17},{9,25},{17,1},{25,9},{2,18},{10... | collective-permute-start | bytes 602120 | tf_op jit(solution)/shard_map/ppermute | solution.py:551
